TPU v7x, 128 devices: a whole 4x4x4 slice. The times are simulated.
128 devices in a mesh: row: 8 (over y_hi, x), col: 16 (over y_lo, z, core).
Axes of the slice: x: 4, y: 4 (y_hi: 2, y_lo: 2; y = y_hi * 2 + y_lo), z: 4, core: 2. Of those that a mesh axis runs over, the one named last changes fastest.
Arguments:
- front_orig: float32 [12288, 12288], P('row', 'col')
- pivot_shift: float32 [12288], replicated, may hold values from 4.5 to 9
- child_update: float32 [16384, 8192], P('row', 'col'), may hold values from -0.046875 to 0.046875
- child_map: int32 [2, 32], replicated, may hold values from 0 to 47, as said below
Outputs:
- front_out: float32 [12288, 12288], P('row', 'col')
Inputs may be any that keep to these rules, and one draw needn't show every extreme that they name: Child h's block b (rows and columns alike) goes to parent block child_map[h, b]; child_map[h, b] % 16 == b % 16; the two child blocks b and b + 16 (b < 16) take two different ones of the parent blocks b, b + 16, b + 32, the smaller child block to the smaller parent block.
All inputs are finite; a program needn't handle non-finite values.
Results may differ from a plain program's by a relative error of at most 0.0001.
Values sent between devices are 32-bit elements; how exact they have to be, the bound alone decides.
No kernel may reach another device: no remote copies, remote signals or barrier semaphores. Data moves between devices by JAX's collectives and lax.ppermute only.
A program may use at most 128 MiB of HBM per device.

v0:
```python
import jax
import jax.numpy as jnp
from jax import lax
from jax.sharding import PartitionSpec as P

BS = 256
PANELS = 6


def from_partner(shard, axis, apart):
    return lax.ppermute(shard, axis, [(i, i ^ 1 << apart) for i in range(lax.axis_size(axis))])


def from_root(shard, axis, root):
    mine = lax.axis_index(axis) == root
    return lax.psum(jnp.where(mine, shard, jnp.zeros_like(shard)), axis)


def symmetric_block(pivot_block):
    return jnp.tril(pivot_block) + jnp.tril(pivot_block, -1).T


def factor_rows(pivot, panel_rows):
    factor = jnp.linalg.cholesky(symmetric_block(pivot))
    below = lax.linalg.triangular_solve(
        factor, panel_rows, left_side=False, lower=True, transpose_a=True
    )
    return (factor, below)


def on_device(front_orig, pivot_shift, child_update, child_map):
    n_row = lax.axis_size("row")
    n_col = lax.axis_size("col")
    row_id = lax.axis_index("row")
    col_id = lax.axis_index("col")
    half_rows = n_row // 2
    local_rows = front_orig.shape[0] // BS
    local_cols = front_orig.shape[1] // BS
    child_rows = child_update.shape[0] // BS
    child_cols = child_update.shape[1] // BS
    pair_count = child_rows // 2
    child_side = row_id // half_rows
    inner_row = row_id % half_rows
    holds_first = child_side == 0
    paired = child_update.reshape(pair_count, 2, BS, child_cols * BS)
    even_blocks = paired[:, 0]
    odd_blocks = paired[:, 1]
    outgoing = jnp.where(holds_first, odd_blocks, even_blocks)
    staying = jnp.where(holds_first, even_blocks, odd_blocks)
    arrived = from_partner(outgoing, "row", half_rows.bit_length() - 1)
    first_part = jnp.where(holds_first, staying, arrived)
    second_part = jnp.where(holds_first, arrived, staying)
    table_index = jnp.arange(child_map.shape[1], dtype=jnp.int32)
    row_wanted = (2 * jnp.arange(pair_count, dtype=jnp.int32) + child_side) * half_rows + inner_row
    col_wanted = jnp.arange(child_cols, dtype=jnp.int32) * n_col + col_id

    def lookup(targets, wanted):
        return jnp.sum(
            jnp.where(wanted[:, None] == table_index[None, :], targets[None, :], 0), axis=1
        )

    def place(part, child_id):
        targets = child_map[child_id]
        row_target = lookup(targets, row_wanted) // n_row
        col_target = lookup(targets, col_wanted) // n_col
        row_pick = (row_target[None, :] == jnp.arange(local_rows, dtype=jnp.int32)[:, None]).astype(
            jnp.float32
        )
        col_pick = (col_target[None, :] == jnp.arange(local_cols, dtype=jnp.int32)[:, None]).astype(
            jnp.float32
        )
        tiles = part.reshape(pair_count, BS, child_cols, BS)
        placed = jnp.einsum(
            "pq,qsjt,kj->pskt", row_pick, tiles, col_pick, precision=lax.Precision.HIGHEST
        )
        return placed.reshape(local_rows * BS, local_cols * BS)

    row_blocks = jnp.arange(local_rows, dtype=jnp.int32) * n_row + row_id
    col_blocks = jnp.arange(local_cols, dtype=jnp.int32) * n_col + col_id
    offsets = jnp.arange(BS, dtype=jnp.int32)
    row_index = (row_blocks[:, None] * BS + offsets[None, :]).reshape(-1)
    col_index = (col_blocks[:, None] * BS + offsets[None, :]).reshape(-1)
    shift_rows = lax.dynamic_index_in_dim(
        pivot_shift.reshape(local_rows, n_row, BS), row_id, axis=1, keepdims=False
    ).reshape(-1)
    diag_term = jnp.where(row_index[:, None] == col_index[None, :], shift_rows[:, None], 0.0)
    front_now = front_orig + diag_term
    front_now = front_now + place(first_part, 0)
    front_now = front_now + place(second_part, 1)
    row_of = jnp.repeat(row_blocks, BS)
    col_of = jnp.repeat(col_blocks, BS)
    stride = n_col // n_row
    pick_index = jnp.arange(local_cols, dtype=jnp.int32) * stride + col_id // n_row
    pick_table = (pick_index[:, None] == jnp.arange(local_rows, dtype=jnp.int32)[None, :]).astype(
        jnp.float32
    )
    level = row_blocks[:, None, None]
    for panel_id in range(PANELS):
        owner_row = panel_id % n_row
        owner_col = panel_id % n_col
        row_slot = panel_id // n_row
        col_slot = panel_id // n_col
        column = front_now[:, col_slot * BS : (col_slot + 1) * BS]
        pivot_local = column[row_slot * BS : (row_slot + 1) * BS]
        pivot = from_root(pivot_local, "row", owner_row)
        factor, own_rows = factor_rows(pivot, column)
        below = from_root(own_rows, "col", owner_col)
        chosen = jnp.einsum(
            "jp,pst->jst",
            pick_table,
            below.reshape(local_rows, BS, BS),
            precision=lax.Precision.HIGHEST,
        )
        across = from_root(chosen.reshape(local_cols * BS, BS), "row", col_id % n_row)
        live = (row_of > panel_id)[:, None] & (col_of > panel_id)[None, :]
        update = jnp.einsum("rk,ck->rc", below, across, precision=lax.Precision.HIGHEST)
        front_now = front_now - jnp.where(live, update, 0.0)
        tiles_now = column.reshape(local_rows, BS, BS)
        below_tiles = below.reshape(local_rows, BS, BS)
        new_column = jnp.where(
            level > panel_id, below_tiles, jnp.where(level == panel_id, factor[None], tiles_now)
        )
        new_column = new_column.reshape(local_rows * BS, BS)
        kept_column = front_now[:, col_slot * BS : (col_slot + 1) * BS]
        front_now = front_now.at[:, col_slot * BS : (col_slot + 1) * BS].set(
            jnp.where(col_id == owner_col, new_column, kept_column)
        )
    return front_now


def solution(mesh):
    in_specs = (P("row", "col"), P(), P("row", "col"), P())
    out_specs = P("row", "col")
    return jax.shard_map(
        on_device, mesh=mesh, in_specs=in_specs, out_specs=out_specs, check_vma=False
    )
```

profile of v0, /device:TPU:10, one launch (start us, length us, event | category | flops | bytes accessed | tf_op | source)
XLA Modules:
  0.0 2398.5 jit_solution(18215019468247353154)
XLA Ops:
  11.9 6.1 copy.296
  18.4 39.9 %collective-permute-done = f32[4,256,512]{2,1,0:T(8,128)} collective-permute-done((f32[4,256,512]{2,1,0:T(8,128)S(1)}, f32[4,256,512]{2,1,0:T(8,128)}, u32[]{:S(2)}, u32[]{:S(2)}) %collective-permute-start) | collective-permute-done | bytes 2097184 | tf_op jit(solution)/shard_map/ppermute | solution.py:11
  58.3 5.2 broadcast_select_fusion.1
  70.1 8.4 fusion.4
  78.4 6.7 copy.304
  85.1 7.4 copy.405
  99.3 8.4 fusion.7
  107.7 6.7 copy.308
  114.3 5.2 copy.406
  126.6 81.7 %all-reduce.20.cloned.1.call-done = f32[256,256]{0,1:T(8,128)} async-done(((f32[256,256]{0,1:T(8,128)}), f32[256,256]{0,1:T(8,128)}) %all-reduce.20.cloned.1.call-update) | async-done | bytes 262160 | tf_op jit(solution)/shard_map/psum | solution.py:16
  210.6 11.7 cholesky.298
  222.4 9.8 custom-call.21
  232.9 11.7 cholesky.315
  247.4 4.5 while.18
  251.9 19.7 custom-call.22
  277.7 123.1 %all-reduce.22.cloned.1.call-done = f32[1536,256]{0,1:T(8,128)} async-done(((f32[1536,256]{0,1:T(8,128)}), f32[1536,256]{0,1:T(8,128)}) %all-reduce.22.cloned.1.call-update) | async-done | bytes 1572880 | tf_op jit(solution)/shard_map/psum | solution.py:16
  408.6 81.0 %all-reduce.24.cloned.1.call-done = f32[768,256]{1,0:T(8,128)} async-done(((f32[768,256]{1,0:T(8,128)}), f32[768,256]{1,0:T(8,128)}) %all-reduce.24.cloned.1.call-update) | async-done | bytes 786448 | tf_op jit(solution)/shard_map/psum | solution.py:16
  489.5 8.0 select_subtract_fusion.5
  497.6 4.3 constant_dynamic-update-slice_fusion.10
  502.8 82.4 %all-reduce.26.cloned.1.call-done = f32[256,256]{0,1:T(8,128)} async-done(((f32[256,256]{0,1:T(8,128)}), f32[256,256]{0,1:T(8,128)}) %all-reduce.26.cloned.1.call-update) | async-done | bytes 262160 | tf_op jit(solution)/shard_map/psum | solution.py:16
  587.5 11.7 cholesky.332
  599.3 9.8 custom-call.23
  609.6 11.7 cholesky.349
  627.9 19.7 custom-call.24
  651.4 123.1 %all-reduce.28.cloned.1.call-done = f32[1536,256]{0,1:T(8,128)} async-done(((f32[1536,256]{0,1:T(8,128)}), f32[1536,256]{0,1:T(8,128)}) %all-reduce.28.cloned.1.call-update) | async-done | bytes 1572880 | tf_op jit(solution)/shard_map/psum | solution.py:16
  784.3 79.0 %all-reduce.30.cloned.1.call-done = f32[768,256]{1,0:T(8,128)} async-done(((f32[768,256]{1,0:T(8,128)}), f32[768,256]{1,0:T(8,128)}) %all-reduce.30.cloned.1.call-update) | async-done | bytes 786448 | tf_op jit(solution)/shard_map/psum | solution.py:16
  863.4 6.7 select_subtract_fusion.4
  878.9 82.1 %all-reduce.32.cloned.1.call-done = f32[256,256]{1,0:T(8,128)} async-done(((f32[256,256]{1,0:T(8,128)}), f32[256,256]{1,0:T(8,128)}) %all-reduce.32.cloned.1.call-update) | async-done | bytes 262160 | tf_op jit(solution)/shard_map/psum | solution.py:16
  963.4 11.7 cholesky.366
  975.2 9.8 custom-call.25
  985.5 11.7 cholesky.383
  999.9 4.2 while.20
  1004.1 19.7 custom-call.26
  1028.3 123.1 %all-reduce.34.cloned.1.call-done = f32[1536,256]{0,1:T(8,128)} async-done(((f32[1536,256]{0,1:T(8,128)}), f32[1536,256]{0,1:T(8,128)}) %all-reduce.34.cloned.1.call-update) | async-done | bytes 1572880 | tf_op jit(solution)/shard_map/psum | solution.py:16
  1160.9 6.2 copy.346
  1167.2 72.9 %all-reduce.36.cloned.1.call-done = f32[768,256]{1,0:T(8,128)} async-done(((f32[768,256]{1,0:T(8,128)}), f32[768,256]{1,0:T(8,128)}) %all-reduce.36.cloned.1.call-update) | async-done | bytes 786448 | tf_op jit(solution)/shard_map/psum | solution.py:16
  1240.1 11.9 select_subtract_fusion.3
  1258.5 82.1 %all-reduce.38.cloned.1.call-done = f32[256,256]{1,0:T(8,128)} async-done(((f32[256,256]{1,0:T(8,128)}), f32[256,256]{1,0:T(8,128)}) %all-reduce.38.cloned.1.call-update) | async-done | bytes 262160 | tf_op jit(solution)/shard_map/psum | solution.py:16
  1342.9 11.7 cholesky.400
  1354.7 9.8 custom-call.27
  1365.0 11.7 cholesky.417
  1379.4 4.1 while.21
  1383.6 19.7 custom-call.28
  1407.7 123.1 %all-reduce.40.cloned.1.call-done = f32[1536,256]{0,1:T(8,128)} async-done(((f32[1536,256]{0,1:T(8,128)}), f32[1536,256]{0,1:T(8,128)}) %all-reduce.40.cloned.1.call-update) | async-done | bytes 1572880 | tf_op jit(solution)/shard_map/psum | solution.py:16
  1536.1 83.5 %all-reduce.42.cloned.1.call-done = f32[768,256]{1,0:T(8,128)} async-done(((f32[768,256]{1,0:T(8,128)}), f32[768,256]{1,0:T(8,128)}) %all-reduce.42.cloned.1.call-update) | async-done | bytes 786448 | tf_op jit(solution)/shard_map/psum | solution.py:16
  1619.6 12.2 select_subtract_fusion.2
  1631.8 4.6 constant_dynamic-update-slice_fusion.7
  1637.6 82.1 %all-reduce.44.cloned.1.call-done = f32[256,256]{1,0:T(8,128)} async-done(((f32[256,256]{1,0:T(8,128)}), f32[256,256]{1,0:T(8,128)}) %all-reduce.44.cloned.1.call-update) | async-done | bytes 262160 | tf_op jit(solution)/shard_map/psum | solution.py:16
  1722.0 11.7 cholesky.434
  1733.8 9.8 custom-call.29
  1744.1 11.7 cholesky.451
  1762.7 19.7 custom-call.30
  1786.8 123.1 %all-reduce.46.cloned.1.call-done = f32[1536,256]{0,1:T(8,128)} async-done(((f32[1536,256]{0,1:T(8,128)}), f32[1536,256]{0,1:T(8,128)}) %all-reduce.46.cloned.1.call-update) | async-done | bytes 1572880 | tf_op jit(solution)/shard_map/psum | solution.py:16
  1915.2 83.4 %all-reduce.48.cloned.1.call-done = f32[768,256]{1,0:T(8,128)} async-done(((f32[768,256]{1,0:T(8,128)}), f32[768,256]{1,0:T(8,128)}) %all-reduce.48.cloned.1.call-update) | async-done | bytes 786448 | tf_op jit(solution)/shard_map/psum | solution.py:16
  1998.7 11.0 select_subtract_fusion.1
  2013.1 82.1 %all-reduce.50.cloned.1.call-done = f32[256,256]{1,0:T(8,128)} async-done(((f32[256,256]{1,0:T(8,128)}), f32[256,256]{1,0:T(8,128)}) %all-reduce.50.cloned.1.call-update) | async-done | bytes 262160 | tf_op jit(solution)/shard_map/psum | solution.py:16
  2097.6 11.7 cholesky.468
  2109.3 9.8 custom-call.31
  2119.6 11.7 cholesky.485
  2134.0 4.2 while.23
  2138.3 19.7 custom-call.32
  2162.5 123.1 %all-reduce.52.cloned.1.call-done = f32[1536,256]{0,1:T(8,128)} async-done(((f32[1536,256]{0,1:T(8,128)}), f32[1536,256]{0,1:T(8,128)}) %all-reduce.52.cloned.1.call-update) | async-done | bytes 1572880 | tf_op jit(solution)/shard_map/psum | solution.py:16
  2292.9 81.5 %all-reduce.54.cloned.1.call-done = f32[768,256]{1,0:T(8,128)} async-done(((f32[768,256]{1,0:T(8,128)}), f32[768,256]{1,0:T(8,128)}) %all-reduce.54.cloned.1.call-update) | async-done | bytes 786448 | tf_op jit(solution)/shard_map/psum | solution.py:16
  2374.3 13.8 select_subtract_fusion
  (350 shorter events, 179.8 us)
Async XLA Ops:
  6.5 201.7 %all-reduce.20.cloned.1.call-start = ((), (), s32[]{:S(2)}) async-start(), calls=%async_computation | async-start | bytes 524288 | tf_op jit(solution)/shard_map/psum | solution.py:16
  6.5 5.1 copy-start.18
  9.2 49.1 %collective-permute-start = (f32[4,256,512]{2,1,0:T(8,128)S(1)}, f32[4,256,512]{2,1,0:T(8,128)}, u32[]{:S(2)}, u32[]{:S(2)}) collective-permute-start(f32[4,256,512]{2,1,0:T(8,128)S(1)} %select_bitcast_fusion), channel_id=1, source_target_pairs={{0,64},{16,80},{32,96},{48,112},{64,0},{80,16},{96,32},{112,48},{1... | collective-permute-start | bytes 6291464 | tf_op jit(solution)/shard_map/ppermute | solution.py:11
  11.9 6.1 copy-start.19
  85.1 7.4 copy-start.11
  114.3 5.3 slice-start
  114.3 5.3 slice-start.1
  122.9 2.2 copy-start
  125.8 275.0 %all-reduce.22.cloned.1.call-start = ((), (), s32[]{:S(2)}) async-start(), calls=%async_computation.1 | async-start | bytes 3145728 | tf_op jit(solution)/shard_map/psum | solution.py:16
  277.6 211.9 %all-reduce.24.cloned.1.call-start = ((), (), s32[]{:S(2)}) async-start(), calls=%async_computation.2 | async-start | bytes 1572864 | tf_op jit(solution)/shard_map/psum | solution.py:16
  405.7 179.5 %all-reduce.26.cloned.1.call-start = ((), (), s32[]{:S(2)}) async-start(), calls=%async_computation.3 | async-start | bytes 524288 | tf_op jit(solution)/shard_map/psum | solution.py:16
  406.9 82.6 %copy-start.9 = (f32[1536,256]{0,1:T(8,128)S(1)}, f32[1536,256]{0,1:T(8,128)}, u32[]{:S(2)}) copy-start(f32[1536,256]{0,1:T(8,128)} %all-reduce.22.cloned.1.call-done) | copy-start | bytes 4718596
  489.5 8.0 copy-start.15
  502.6 272.0 %all-reduce.28.cloned.1.call-start = ((), (), s32[]{:S(2)}) async-start(), calls=%async_computation.4 | async-start | bytes 3145728 | tf_op jit(solution)/shard_map/psum | solution.py:16
  651.4 212.0 %all-reduce.30.cloned.1.call-start = ((), (), s32[]{:S(2)}) async-start(), calls=%async_computation.5 | async-start | bytes 1572864 | tf_op jit(solution)/shard_map/psum | solution.py:16
  779.6 181.5 %all-reduce.32.cloned.1.call-start = ((), (), s32[]{:S(2)}) async-start(), calls=%async_computation.6 | async-start | bytes 524288 | tf_op jit(solution)/shard_map/psum | solution.py:16
  781.2 82.2 %copy-start.10 = (f32[1536,256]{0,1:T(8,128)S(1)}, f32[1536,256]{0,1:T(8,128)}, u32[]{:S(2)}) copy-start(f32[1536,256]{0,1:T(8,128)} %all-reduce.28.cloned.1.call-done) | copy-start | bytes 4718596
  863.4 6.7 copy-start.16
  870.1 3.1 copy-start.3
  873.3 2.0 copy-start.17
  878.5 272.9 %all-reduce.34.cloned.1.call-start = ((), (), s32[]{:S(2)}) async-start(), calls=%async_computation.7 | async-start | bytes 3145728 | tf_op jit(solution)/shard_map/psum | solution.py:16
  1028.3 211.9 %all-reduce.36.cloned.1.call-start = ((), (), s32[]{:S(2)}) async-start(), calls=%async_computation.8 | async-start | bytes 1572864 | tf_op jit(solution)/shard_map/psum | solution.py:16
  1156.3 184.3 %all-reduce.38.cloned.1.call-start = ((), (), s32[]{:S(2)}) async-start(), calls=%async_computation.9 | async-start | bytes 524288 | tf_op jit(solution)/shard_map/psum | solution.py:16
  1253.9 2.2 copy-start.2
  1256.1 1.2 copy-start.6
  1258.0 272.9 %all-reduce.40.cloned.1.call-start = ((), (), s32[]{:S(2)}) async-start(), calls=%async_computation.10 | async-start | bytes 3145728 | tf_op jit(solution)/shard_map/psum | solution.py:16
  1342.9 60.4 %copy-start.7 = (f32[1536,256]{1,0:T(8,128)S(1)}, f32[1536,256]{1,0:T(8,128)}, u32[]{:S(2)}) copy-start(f32[1536,256]{1,0:T(8,128)} %copy-done.6) | copy-start | bytes 4718596
  1407.7 211.9 %all-reduce.42.cloned.1.call-start = ((), (), s32[]{:S(2)}) async-start(), calls=%async_computation.11 | async-start | bytes 1572864 | tf_op jit(solution)/shard_map/psum | solution.py:16
  1534.7 84.9 %copy-start.12 = (f32[1536,256]{0,1:T(8,128)S(1)}, f32[1536,256]{0,1:T(8,128)}, u32[]{:S(2)}) copy-start(f32[1536,256]{0,1:T(8,128)} %all-reduce.40.cloned.1.call-done) | copy-start | bytes 4718596
  1535.8 183.9 %all-reduce.44.cloned.1.call-start = ((), (), s32[]{:S(2)}) async-start(), calls=%async_computation.12 | async-start | bytes 524288 | tf_op jit(solution)/shard_map/psum | solution.py:16
  1619.6 12.2 copy-start.8
  1636.3 146.9 %copy-start.4 = (f32[1536,256]{1,0:T(8,128)}, f32[1536,256]{1,0:T(8,128)S(1)}, u32[]{:S(2)}) copy-start(f32[1536,256]{1,0:T(8,128)S(1)} %get-tuple-element.244) | copy-start | bytes 4718596
  1637.1 272.8 %all-reduce.46.cloned.1.call-start = ((), (), s32[]{:S(2)}) async-start(), calls=%async_computation.13 | async-start | bytes 3145728 | tf_op jit(solution)/shard_map/psum | solution.py:16
  1786.8 211.9 %all-reduce.48.cloned.1.call-start = ((), (), s32[]{:S(2)}) async-start(), calls=%async_computation.14 | async-start | bytes 1572864 | tf_op jit(solution)/shard_map/psum | solution.py:16
  1913.8 84.9 %copy-start.13 = (f32[1536,256]{0,1:T(8,128)S(1)}, f32[1536,256]{0,1:T(8,128)}, u32[]{:S(2)}) copy-start(f32[1536,256]{0,1:T(8,128)} %all-reduce.46.cloned.1.call-done) | copy-start | bytes 4718596
  1914.9 180.3 %all-reduce.50.cloned.1.call-start = ((), (), s32[]{:S(2)}) async-start(), calls=%async_computation.15 | async-start | bytes 524288 | tf_op jit(solution)/shard_map/psum | solution.py:16
  1998.7 11.1 copy-start.5
  2009.7 2.2 copy-start.1
  2012.6 273.0 %all-reduce.52.cloned.1.call-start = ((), (), s32[]{:S(2)}) async-start(), calls=%async_computation.16 | async-start | bytes 3145728 | tf_op jit(solution)/shard_map/psum | solution.py:16
  2162.4 211.9 %all-reduce.54.cloned.1.call-start = ((), (), s32[]{:S(2)}) async-start(), calls=%async_computation.17 | async-start | bytes 1572864 | tf_op jit(solution)/shard_map/psum | solution.py:16
  2374.3 13.8 copy-start.14
Sparse Core Ops, SparseCore 0:
  126.0 82.2 all-reduce.19
  277.8 123.0 all-reduce.21
  405.8 83.6 all-reduce.23
  502.7 82.4 all-reduce.25
  651.5 123.0 all-reduce.27
  779.7 83.6 all-reduce.29
  878.6 82.3 all-reduce.31
  1028.4 123.0 all-reduce.33
  1156.4 83.6 all-reduce.35
  1258.1 82.3 all-reduce.37
  1407.8 123.0 all-reduce.39
  1535.9 83.6 all-reduce.41
  1637.2 82.4 all-reduce.43
  1786.9 123.0 all-reduce.45
  1915.0 83.6 all-reduce.47
  2012.8 82.3 all-reduce.49
  2162.5 123.0 all-reduce.51
  2290.6 83.6 all-reduce.53
where the time goes:
time: 2410 us; the launch traced here: 2400 us
  waiting for transfers between devices  1750 us (73%)
  other arithmetic  380 us (16%)
  matrix products  120 us (5%)
  local copies, waits for them, and re-layouts  117 us (5%)
    psum x18, waiting for transfers between devices, from_root(): return lax.psum(jnp.where(mine, shard, jnp.zeros_like(shard)), axis)  1710 us
    another operation x42, other arithmetic, factor_rows(): factor = jnp.linalg.cholesky(symmetric_block(pivot))  208 us
    another operation x13, other arithmetic, factor_rows(): lax.linalg.triangular_solve(factor, panel_rows, left_side=False, lower=Tr...  118 us
    dot_general x6, matrix products, on_device(): jnp.einsum('rk,ck->rc', below, across, precision=lax.Precision.HIGHEST)  63.6 us
  transfers between devices with their start and end apart: 19, of which 19 were waited for; matrix products, arithmetic and copies ran while one was open for 1% of the time, Pallas kernels for 0%

commit v1 on v0

v1 whole, which is shorter than its diff:
```python
import jax
import jax.numpy as jnp
from jax import lax
from jax.experimental import pallas as pl
from jax.experimental.pallas import tpu as pltpu
from jax.sharding import PartitionSpec as P

PANELS = 6
BS=256
NT = (((1,), (1,)), ((), ()))
NN = (((1,), (0,)), ((), ()))

def split(x):
    hi = x.astype(jnp.bfloat16)
    return hi, (x - hi.astype(jnp.float32)).astype(jnp.bfloat16)

def dot(a, b, dims=NT):
    return lax.dot_general(a, b, dims, preferred_element_type=jnp.float32)

def dot3(ah, al, bh, bl, dims=NT):
    return dot(ah, bh, dims) + (dot(ah, bl, dims) + dot(al, bh, dims))

def mul3(a, b, dims=NT):
    return dot3(*split(a), *split(b), dims)

def leaf(sym):
    n = sym.shape[0]
    groups = n // 8
    lane = lax.broadcasted_iota(jnp.int32, (8, n), 1)
    sub = lax.broadcasted_iota(jnp.int32, (8, n), 0)
    across = lambda v, j: jnp.broadcast_to(v[:, j:j + 1], (8, n))
    down = lambda v, s: jnp.broadcast_to(v[s:s + 1, :], (8, n))
    rows = [sym[8 * h:8 * h + 8] for h in range(groups)]
    right = [jnp.where(lane == sub + 8 * h, 1.0, 0.0) for h in range(groups)]
    upper, inverse = [], []
    for g in range(groups):
        cols = [across(rows[g], 8 * g + t) for t in range(8)]
        a = {(s, t): down(cols[t], s) for t in range(8) for s in range(t, 8)}
        u = [down(rows[g], t) for t in range(8)]
        w = [down(right[g], t) for t in range(8)]
        later = range(g + 1, groups)
        x = {h: [across(rows[h], 8 * g + t) for t in range(8)] for h in later}
        for t in range(8):
            r = lax.rsqrt(a[t, t])
            for s in range(t + 1, 8):
                a[s, t] = a[s, t] * r
            u[t] = u[t] * r
            w[t] = w[t] * r
            for h in later:
                x[h][t] = x[h][t] * r
            for s in range(t + 1, 8):
                for v in range(t + 1, s + 1):
                    a[s, v] = a[s, v] - a[s, t] * a[v, t]
                u[s] = u[s] - a[s, t] * u[t]
                w[s] = w[s] - a[s, t] * w[t]
                for h in later:
                    x[h][s] = x[h][s] - a[s, t] * x[h][t]
        for h in later:
            for t in range(8):
                rows[h] = rows[h] - x[h][t] * u[t]
                right[h] = right[h] - x[h][t] * w[t]
        ug, wg = u[0], w[0]
        for t in range(1, 8):
            ug = jnp.where(sub == t, u[t], ug)
            wg = jnp.where(sub == t, w[t], wg)
        upper.append(jnp.where(lane >= sub + 8 * g, ug, 0.0))
        inverse.append(wg)
    return jnp.concatenate(upper, axis=0).T, jnp.concatenate(inverse, axis=0)

def symmetric(d):
    n = d.shape[0]
    below = lax.broadcasted_iota(jnp.int32, (n, n), 0) >= lax.broadcasted_iota(jnp.int32, (n, n), 1)
    return jnp.where(below, d, d.T)

LEAF = 128
def chol_kernel(panels, top_ref, lh_ref, ll_ref, ih_ref, il_ref, fac_ref, a_ref, s_ref, f_ref, w_ref):
    e = 0
    for i in range(panels):
        for k in range(i + 1):
            a_ref[k * panels + i] = top_ref[:, e].reshape(BS, BS)
            e += 1
    zero = jnp.zeros((LEAF, LEAF), jnp.float32)

    def panel(k, carry):
        d = a_ref[k * panels + k]
        s_ref[0] = d[:LEAF, :LEAF]
        s_ref[1] = d[LEAF:, LEAF:]
        s_ref[2] = d[LEAF:, :LEAF]

        def half(h, carry):
            factor, inverse = leaf(symmetric(s_ref[h]))
            f_ref[h] = factor
            w_ref[h] = inverse

            @pl.when(h == 0)
            def _():
                low = mul3(s_ref[2], inverse)
                s_ref[2] = low
                s_ref[1] = s_ref[1] - mul3(low, low)
            return carry
        lax.fori_loop(0, 2, half, 0)
        corner = -mul3(w_ref[1], mul3(s_ref[2], w_ref[0], NN), NN)
        fac_ref[k] = jnp.concatenate([jnp.concatenate([f_ref[0], zero], 1), jnp.concatenate([s_ref[2], f_ref[1]], 1)], 0)
        inv = jnp.concatenate([jnp.concatenate([w_ref[0], zero], 1), jnp.concatenate([corner, w_ref[1]], 1)], 0)
        ih, il = split(inv)
        ih_ref[k] = ih
        il_ref[k] = il
        for at in range(panels - 1):
            @pl.when(k == at)
            def _(at=at):
                rest = panels - 1 - at
                below = a_ref[at * panels + at + 1:(at + 1) * panels].reshape(rest * BS, BS)
                xh, xl = split(dot3(*split(below), ih, il))
                lh_ref[at, at + 1:] = xh.reshape(rest, BS, BS)
                ll_ref[at, at + 1:] = xl.reshape(rest, BS, BS)
                for j in range(at + 1, panels):
                    o = (j - at - 1) * BS
                    old = a_ref[j * panels + j:(j + 1) * panels]
                    upd = dot3(xh[o:], xl[o:], xh[o:o + BS], xl[o:o + BS])
                    a_ref[j * panels + j:(j + 1) * panels] = old - upd.reshape(panels - j, BS, BS)
        return carry
    lax.fori_loop(0, panels, panel, 0)

def chol(top, panels=6):
    f32, bf = jnp.float32, jnp.bfloat16
    return pl.pallas_call(
        lambda *refs: chol_kernel(panels, *refs),
        out_shape=[jax.ShapeDtypeStruct((panels, panels, BS, BS), bf)] * 2 + [jax.ShapeDtypeStruct((panels, BS, BS), bf)] * 2 + [jax.ShapeDtypeStruct((panels, BS, BS), f32)],
        scratch_shapes=[pltpu.VMEM((panels * panels, BS, BS), f32), pltpu.VMEM((3, LEAF, LEAF), f32), pltpu.VMEM((2, LEAF, LEAF), f32), pltpu.VMEM((2, LEAF, LEAF), f32)],
        compiler_params=pltpu.CompilerParams(vmem_limit_bytes=56 * 2**20),
        name="top",
    )(top)

HALF_ROWS = 4
N_ROW = 8
N_COL = 16
STRIP = BS // N_COL
CHUNK = BS // N_ROW
ROW_SLOTS = 6
COL_SLOTS = 3
ROW_TILE = 2


def solve_rows(x_ref, f_ref, h_ref, l_ref, rows, lh_ref, ll_ref, ih_ref, il_ref):
    for k in range(PANELS):
        acc = x_ref[k, :rows]
        for m in range(k):
            acc = acc - dot3(h_ref[m, :rows], l_ref[m, :rows], lh_ref[m, k], ll_ref[m, k])
        out = dot3(*split(acc), ih_ref[k], il_ref[k])
        hi, lo = split(out)
        h_ref[k, :rows] = hi
        l_ref[k, :rows] = lo
        if f_ref is not None:
            f_ref[k, :rows] = out


def rows_kernel(place_ref, row_ref, *refs):
    pieces = refs[:N_ROW]
    lh_ref, ll_ref, ih_ref, il_ref, fac_ref, front_ref, out_ref, x_ref, f_ref, rh_ref, rl_ref, ch_ref, cl_ref = refs[N_ROW:]
    r, c = place_ref[0], place_ref[1]
    step = pl.program_id(0)
    blank = jnp.zeros((BS, BS), jnp.bfloat16)

    @pl.when(step == 0)
    def _():
        for m in range(N_ROW):
            at = (r ^ m) * CHUNK
            for k in range(PANELS):
                for s in range(COL_SLOTS):
                    x_ref[k, pl.ds(pl.multiple_of(s * BS + at, CHUNK), CHUNK)] = pieces[m][k, s]
        solve_rows(x_ref, None, ch_ref, cl_ref, COL_SLOTS * BS, lh_ref, ll_ref, ih_ref, il_ref)
        for k in range(PANELS):
            @pl.when(k >= c)
            def _(k=k):
                ch_ref[k, :BS] = blank
                cl_ref[k, :BS] = blank

    @pl.when(step > 0)
    def _():
        rows = ROW_TILE * BS
        for k in range(PANELS):
            for s in range(ROW_TILE):
                x_ref[k, s * BS:(s + 1) * BS] = row_ref[:, k, s].reshape(BS, BS)
        solve_rows(x_ref, f_ref, rh_ref, rl_ref, rows, lh_ref, ll_ref, ih_ref, il_ref)

        @pl.when(step == 1)
        def _():
            for k in range(PANELS):
                @pl.when(k >= r)
                def _(k=k):
                    rh_ref[k, :BS] = blank
                    rl_ref[k, :BS] = blank
        acc = front_ref[...]
        for k in range(PANELS):
            acc = acc - dot3(rh_ref[k], rl_ref[k], ch_ref[k], cl_ref[k])
        out_ref[...] = acc

        @pl.when(c < PANELS)
        def _():
            for s in range(ROW_TILE):
                level = ((step - 1) * ROW_TILE + s) * N_ROW + r

                @pl.when(level > c)
                def _(s=s):
                    out_ref[s * BS:(s + 1) * BS, :BS] = f_ref[c, s * BS:(s + 1) * BS]

                @pl.when(level == c)
                def _(s=s):
                    out_ref[s * BS:(s + 1) * BS, :BS] = fac_ref[c]


def finish(place, row_panel, pieces, lh, ll, ih, il, fac, front):
    f32, bf = jnp.float32, jnp.bfloat16
    tiles = ROW_SLOTS // ROW_TILE
    whole = pl.BlockSpec(memory_space=pltpu.VMEM)
    tile_at = lambda g: jnp.maximum(g - 1, 0)
    rows, cols = ROW_TILE * BS, COL_SLOTS * BS
    front_spec = pl.BlockSpec((rows, cols), lambda g: (tile_at(g), 0))
    return pl.pallas_call(
        rows_kernel,
        grid=(tiles + 1,),
        in_specs=[
            pl.BlockSpec(memory_space=pltpu.SMEM),
            pl.BlockSpec((N_COL, PANELS, ROW_TILE, STRIP, BS), lambda g: (0, 0, tile_at(g), 0, 0)),
        ]
        + [whole] * N_ROW
        + [whole] * 5
        + [front_spec],
        out_specs=front_spec,
        out_shape=jax.ShapeDtypeStruct(front.shape, f32),
        scratch_shapes=[
            pltpu.VMEM((PANELS, cols, BS), f32),
            pltpu.VMEM((PANELS, rows, BS), f32),
            pltpu.VMEM((PANELS, rows, BS), bf),
            pltpu.VMEM((PANELS, rows, BS), bf),
            pltpu.VMEM((PANELS, cols, BS), bf),
            pltpu.VMEM((PANELS, cols, BS), bf),
        ],
        compiler_params=pltpu.CompilerParams(vmem_limit_bytes=60 * 2**20),
        name="finish",
    )(place, row_panel, *pieces, lh, ll, ih, il, fac, front)


def device(r, c):
    return r * N_COL + c


def permute(x, pairs):
    return lax.ppermute(x, ("row", "col"), pairs)


def swap_rows(x, apart, cols):
    return permute(x, [(device(r, c), device(r ^ apart, c)) for r in range(N_ROW) for c in cols])


def on_device(front_orig, pivot_shift, child_update, child_map):
    r = lax.axis_index("row")
    c = lax.axis_index("col")
    first = r < HALF_ROWS
    owner = c < PANELS

    child = child_update.reshape(4, 2, BS, 2, BS)
    outgoing = jnp.where(first, child[:, 1], child[:, 0])
    staying = jnp.where(first, child[:, 0], child[:, 1])
    lead, tail = outgoing[:, :, 0], outgoing[:, :, 1]
    lead_in = swap_rows(lead, HALF_ROWS, range(PANELS))
    lead_late = swap_rows(lead, HALF_ROWS, range(PANELS, N_COL))
    tail_in = swap_rows(tail, HALF_ROWS, range(N_COL))

    entry = jnp.arange(child_map.shape[1], dtype=jnp.int32)
    want_row = jnp.arange(4, dtype=jnp.int32) * N_ROW + r
    want_col = jnp.arange(2, dtype=jnp.int32) * N_COL + c

    def lookup(wanted):
        hit = wanted[None, :, None] == entry[None, None, :]
        return jnp.sum(jnp.where(hit, child_map[:, None, :], 0), axis=2)

    row_at = lookup(want_row) // N_ROW
    col_at = lookup(want_col) // N_COL

    def put_rows(part, h, slot):
        total = jnp.zeros(part.shape[1:], jnp.float32)
        for q in range(4):
            if slot % 2 == q % 2 and 0 <= slot - q <= 2:
                total = jnp.where(row_at[h, q] == slot, part[q], total)
        return total

    shift = lax.dynamic_index_in_dim(pivot_shift.reshape(ROW_SLOTS, N_ROW, BS), r, axis=1, keepdims=False)
    eye = lax.broadcasted_iota(jnp.int32, (BS, BS), 0) == lax.broadcasted_iota(jnp.int32, (BS, BS), 1)

    def with_shift(tile, p, s):
        on_diagonal = eye & (p * N_ROW + r == s * N_COL + c)
        return tile + jnp.where(on_diagonal, shift[p][:, None], 0.0)

    def front_tile(p, s):
        return with_shift(front_orig[p * BS:(p + 1) * BS, s * BS:(s + 1) * BS], p, s)

    def child_part(h, side, arrived):
        return jnp.where(first == (h == 0), side, arrived)

    column = []
    for p in range(ROW_SLOTS):
        tile = front_tile(p, 0)
        for h in range(2):
            part = child_part(h, staying[:, :, 0], lead_in)
            tile = tile + jnp.where(col_at[h, 0] == 0, put_rows(part, h, p), 0.0)
        column.append(tile)

    strips = lax.all_to_all(column[0].reshape(N_COL, STRIP, BS), "col", 0, 0)[:PANELS]
    near = [strips] + [
        permute(strips, [(device(i, k), device(i ^ m, k)) for i in range(PANELS) for k in range(N_COL)])
        for m in range(1, N_ROW)
    ]
    near = jnp.stack(near)
    packed = jnp.concatenate(
        [lax.dynamic_index_in_dim(near, r ^ i, 0, keepdims=False)[: i + 1] for i in range(PANELS)], axis=0
    )
    top = lax.all_gather(packed, "col")

    column = jnp.stack(column)
    row_part = column[1:].reshape(ROW_SLOTS - 1, N_COL, STRIP, BS).transpose(1, 0, 2, 3)
    row_part = row_part.reshape(N_COL, (ROW_SLOTS - 1) * STRIP, BS)
    col_part = column.reshape(COL_SLOTS, 2, N_ROW, CHUNK, BS).transpose(1, 2, 0, 3, 4)
    col_part = col_part.reshape(N_COL, COL_SLOTS * CHUNK, BS)
    cut = (ROW_SLOTS - 1) * STRIP
    dealt = lax.all_to_all(jnp.concatenate([row_part, col_part], axis=1), "col", 0, 0)[:PANELS]
    row_piece = jnp.concatenate(
        [strips[:, None], dealt[:, :cut].reshape(PANELS, ROW_SLOTS - 1, STRIP, BS)], axis=1
    )
    row_panel = lax.all_gather(row_piece, "col")
    col_piece = dealt[:, cut:].reshape(PANELS, COL_SLOTS, CHUNK, BS)
    col_piece = permute(
        col_piece,
        [
            (device(i, h * N_ROW + j), device(j, h * N_ROW + i))
            for i in range(N_ROW)
            for j in range(N_ROW)
            for h in range(2)
        ],
    )
    pieces = [col_piece] + [swap_rows(col_piece, m, range(N_COL)) for m in range(1, N_ROW)]

    factored = chol(top)

    lead_all = jnp.where(owner, lead_in, lead_late)
    tiles = []
    for p in range(ROW_SLOTS):
        line = []
        for s in range(COL_SLOTS):
            tile = front_tile(p, s)
            for h in range(2):
                here = child_part(h, staying[:, :, 0], lead_all)
                there = child_part(h, staying[:, :, 1], tail_in)
                a = put_rows(here, h, p) if s < 2 else None
                b = put_rows(there, h, p) if s > 0 else None
                extra = jnp.zeros_like(tile)
                if a is not None:
                    extra = jnp.where(col_at[h, 0] == s, a, extra)
                if b is not None:
                    extra = jnp.where(col_at[h, 1] == s, b, extra)
                tile = tile + extra
            line.append(tile)
        tiles.append(jnp.concatenate(line, axis=1))
    front = jnp.concatenate(tiles, axis=0)
    place = jnp.stack([r, c]).astype(jnp.int32)
    return finish(place, row_panel, pieces, *factored, front)


def solution(mesh):
    in_specs = (P("row", "col"), P(), P("row", "col"), P())
    out_specs = P("row", "col")
    return jax.shard_map(
        on_device, mesh=mesh, in_specs=in_specs, out_specs=out_specs, check_vma=False
    )
```

time: 2410 us -> 423 us (0.18)
  waiting for transfers between devices: 1750 us -> 55.7 us
  other arithmetic: 380 us -> 41.4 us
  matrix products: 120 us -> 0 us
  Pallas kernels: 0 us -> 116 us
  local copies, waits for them, and re-layouts: 117 us -> 24.6 us
  starting transfers between devices: 5.09 us -> 94.1 us
  blocking collectives: 0 us -> 55 us
    psum x18 -> x0, waiting for transfers between devices: 1710 us -> none  [from_root(): return lax.psum(jnp.where(mine, shard, jnp.zeros_like(shard)), axis)]
    another operation x56 -> x2, other arithmetic: 327 us -> 2.41 us  [the longest x1 1.76 us: on_device(): column = jnp.stack(column)]
    pallas_call x0 -> x2, Pallas kernels: none -> 116 us  [the longest x1 71 us: chol(): pl.pallas_call(lambda *refs: chol_kernel(panels, *refs), out_shape=[jax.S...]
    dot_general x16 -> x0, matrix products: 97.1 us -> none  [the longest x6 63.6 us: on_device(): jnp.einsum('rk,ck->rc', below, across, precision=lax.Precision.HIGHEST)]
    ppermute x1 -> x18, starting transfers between devices: 2.37 us -> 87.3 us  [permute(): return lax.ppermute(x, ('row', 'col'), pairs)]
    all_to_all x0 -> x1, blocking collectives: none -> 55 us  [on_device(): lax.all_to_all(jnp.concatenate([row_part, col_part], axis=1), 'col', 0, 0)]
    ppermute x1 -> x18, waiting for transfers between devices: 39.9 us -> 48.9 us  [permute(): return lax.ppermute(x, ('row', 'col'), pairs)]
  transfers between devices with their start and end apart: 19 -> 21, of which waited for: 19 -> 6; matrix products, arithmetic and copies ran while one was open for 1% -> 9% of each run, Pallas kernels for 0% -> 17%
where the time goes in v1:
time: 423 us; the launch traced here: 415 us
  Pallas kernels  116 us (27%)
  starting transfers between devices  94.1 us (22%)
  waiting for transfers between devices  55.7 us (13%)
  blocking collectives  55 us (13%)
  other arithmetic  41.4 us (10%)
  between operations  28.9 us (7%)
  local copies, waits for them, and re-layouts  24.6 us (6%)
    ppermute x18, starting transfers between devices, permute(): return lax.ppermute(x, ('row', 'col'), pairs)  87.3 us
    pallas_call x1, Pallas kernels, chol(): pl.pallas_call(lambda *refs: chol_kernel(panels, *refs), out_shape=[jax.S...  71 us
    all_to_all x1, blocking collectives, on_device(): lax.all_to_all(jnp.concatenate([row_part, col_part], axis=1), 'col', 0, 0)  55 us
    ppermute x18, waiting for transfers between devices, permute(): return lax.ppermute(x, ('row', 'col'), pairs)  48.9 us
    pallas_call x1, Pallas kernels, finish(): pl.pallas_call(rows_kernel, grid=(tiles + 1,), in_specs=[pl.BlockSpec(mem...  44.9 us
    unnamed x10, other arithmetic  14.3 us
    add x12, other arithmetic, on_device(): tile = tile + extra  14 us
  transfers between devices with their start and end apart: 21, of which 6 were waited for; matrix products, arithmetic and copies ran while one was open for 9% of the time, Pallas kernels for 17%

profile of v1, /device:TPU:10, one launch (start us, length us, event | category | flops | bytes accessed | tf_op | source)
XLA Modules:
  0.0 415.4 jit_solution(6297843262039584098)
XLA Ops:
  6.5 5.9 %reshape.468 = f32[4,2,256,2,256]{4,3,2,1,0:T(2,128)} reshape(f32[2048,512]{1,0:T(8,128)} %param.6) | data formatting | bytes 8388608 | tf_op jit(solution)/shard_map/reshape | solution.py:262
  12.4 5.6 %fusion.26 = (f32[4,1,256,2,256]{4,3,2,1,0:T(2,128)}, f32[4,1,256,2,256]{4,3,2,1,0:T(2,128)}) fusion(f32[4,2,256,2,256]{4,3,2,1,0:T(2,128)} %reshape.468), kind=kLoop, calls=%fused_computation.170 | loop fusion | bytes 8388608 | tf_op jit(solution)/shard_map/slice | solution.py:264
  18.0 4.1 select_bitcast_fusion.1
  22.1 1.5 slice_bitcast_fusion
  23.6 0.7 collective-permute-start
  24.3 4.2 %collective-permute-start.16 = (f32[4,256,256]{2,1,0:T(8,128)}, f32[4,256,256]{2,1,0:T(8,128)S(1)}, u32[]{:S(2)}, u32[]{:S(2)}) collective-permute-start(f32[4,256,256]{2,1,0:T(8,128)} %get-tuple-element.52), channel_id=1, source_target_pairs={{6,70},{7,71},{8,72},{9,73},{10,74},{11,75},{12,76},{13,77},{14,78... | collective-permute-start | bytes 3145736 | tf_op jit(solution)/shard_map/ppermute | solution.py:249
  28.5 1.3 collective-permute-start.17
  32.2 0.7 fusion.29
  34.3 19.7 %collective-permute-done.16 = f32[4,256,256]{2,1,0:T(8,128)S(1)} collective-permute-done((f32[4,256,256]{2,1,0:T(8,128)}, f32[4,256,256]{2,1,0:T(8,128)S(1)}, u32[]{:S(2)}, u32[]{:S(2)}) %collective-permute-start.16) | collective-permute-done | bytes 1048608 | tf_op jit(solution)/shard_map/ppermute | solution.py:249
  54.0 21.3 %collective-permute-done.17 = f32[4,256,256]{2,1,0:T(8,128)S(1)} collective-permute-done((f32[4,256,256]{2,1,0:T(8,128)}, f32[4,256,256]{2,1,0:T(8,128)S(1)}, u32[]{:S(2)}, u32[]{:S(2)}) %collective-permute-start.17) | collective-permute-done | bytes 1048608 | tf_op jit(solution)/shard_map/ppermute | solution.py:249
  75.3 1.0 copy-done.8
  76.3 4.0 fusion.2
  80.3 1.0 copy-done.1
  81.3 1.9 bitcast_dynamic-update-slice_fusion.5
  83.2 6.8 %all-to-all-start = ((f32[16,16,256]{2,1,0:T(8,128)}), f32[16,16,256]{2,1,0:T(8,128)S(1)}, u32[]{:S(2)}, u32[]{:S(2)}) async-start(f32[16,16,256]{2,1,0:T(8,128)} %bitcast.13), calls=%async_computation | async-start | bytes 524288 | tf_op jit(solution)/shard_map/all_to_all | solution.py:309
  90.0 6.7 %all-to-all-done = f32[16,16,256]{2,1,0:T(8,128)S(1)} async-done(((f32[16,16,256]{2,1,0:T(8,128)}), f32[16,16,256]{2,1,0:T(8,128)S(1)}, u32[]{:S(2)}, u32[]{:S(2)}) %all-to-all-start) | async-done | bytes 262176 | tf_op jit(solution)/shard_map/all_to_all | solution.py:309
  96.8 2.4 collective-permute-start.9
  99.2 4.3 %collective-permute-start.10 = (f32[6,16,256]{2,1,0:T(8,128)S(1)}, f32[6,16,256]{2,1,0:T(8,128)S(1)}, u32[]{:S(2)}, u32[]{:S(2)}) collective-permute-start(f32[6,16,256]{2,1,0:T(8,128)S(1)} %get-tuple-element.53), channel_id=1, source_target_pairs={{0,32},{1,33},{2,34},{3,35},{4,36},{5,37},{6,38},{7,39},{8,40},{9,... | collective-permute-start | bytes 294920 | tf_op jit(solution)/shard_map/ppermute | solution.py:249
  103.6 2.4 collective-permute-start.11
  106.0 1.9 collective-permute-start.12
  108.0 6.6 %collective-permute-start.13 = (f32[6,16,256]{2,1,0:T(8,128)S(1)}, f32[6,16,256]{2,1,0:T(8,128)S(1)}, u32[]{:S(2)}, u32[]{:S(2)}) collective-permute-start(f32[6,16,256]{2,1,0:T(8,128)S(1)} %get-tuple-element.53), channel_id=1, source_target_pairs={{0,80},{1,81},{2,82},{3,83},{4,84},{5,85},{6,86},{7,87},{8,88},{9,... | collective-permute-start | bytes 294920 | tf_op jit(solution)/shard_map/ppermute | solution.py:249
  114.6 1.3 collective-permute-start.14
  115.9 1.3 collective-permute-start.15
  117.3 0.8 collective-permute-done.13
  118.1 1.3 collective-permute-done.15
  121.9 0.6 fusion.24
  132.0 2.1 bitcast_dynamic-update-slice_fusion.4
  134.1 2.1 bitcast_dynamic-update-slice_fusion.3
  136.2 1.8 bitcast_dynamic-update-slice_fusion.2
  137.9 1.8 bitcast_dynamic-update-slice_fusion.1
  139.7 1.8 bitcast_dynamic-update-slice_fusion
  141.5 1.6 copy.30
  143.4 55.0 %all_to_all.10 = f32[16,176,256]{2,1,0:T(8,128)S(1)} all-to-all(f32[16,176,256]{2,1,0:T(8,128)S(1)} %pad_maximum_fusion), channel_id=1, replica_groups=mesh['row'=8,'col'=16] {'col'}, dimensions={0} | all-to-all | bytes 5767168 | tf_op jit(solution)/shard_map/all_to_all | solution.py:326
  198.4 1.6 copy-done.5
  200.0 0.9 pad_maximum_fusion.1
  204.6 0.7 pad_add_fusion.place_ref
  205.2 1.2 bitcast_add_fusion.24
  206.4 1.3 bitcast_add_fusion.34
  207.7 1.0 maximum_dynamic-update-slice_fusion.5
  208.7 1.1 bitcast_add_fusion.22
  209.8 1.1 bitcast_add_fusion.16
  210.8 1.1 bitcast_add_fusion.18
  211.9 1.1 bitcast_add_fusion.12
  213.0 1.3 bitcast_add_fusion.28
  214.3 1.1 slice.265
  215.4 2.3 collective-permute-start.1
  217.7 0.9 maximum_dynamic-update-slice_fusion.4
  218.6 1.2 bitcast_add_fusion
  219.8 1.1 bitcast_add_fusion.20
  221.0 5.7 %collective-permute-done.1.refs_0_ = f32[6,3,32,256]{3,2,1,0:T(8,128)} collective-permute-done((f32[6,3,32,256]{3,2,1,0:T(8,128)S(1)}, f32[6,3,32,256]{3,2,1,0:T(8,128)}, u32[]{:S(2)}, u32[]{:S(2)}) %collective-permute-start.1) | collective-permute-done | bytes 589856 | tf_op jit(solution)/shard_map/ppermute | solution.py:249
  226.7 18.1 %collective-permute-start.3 = (f32[6,3,32,256]{3,2,1,0:T(8,128)}, f32[6,3,32,256]{3,2,1,0:T(8,128)S(1)}, u32[]{:S(2)}, u32[]{:S(2)}) collective-permute-start(f32[6,3,32,256]{3,2,1,0:T(8,128)} %collective-permute-done.1.refs_0_), channel_id=1, source_target_pairs={{0,32},{1,33},{2,34},{3,35},{4,36},{5,37},{6,38},{7,39},{8,40},{9,... | collective-permute-start | bytes 1769480 | tf_op jit(solution)/shard_map/ppermute | solution.py:249
  244.8 1.0 maximum_dynamic-update-slice_fusion.3
  245.8 1.1 bitcast_add_fusion.14
  246.9 1.3 bitcast_add_fusion.10
  248.8 16.7 %collective-permute-start.5 = (f32[6,3,32,256]{3,2,1,0:T(8,128)}, f32[6,3,32,256]{3,2,1,0:T(8,128)}, u32[]{:S(2)}, u32[]{:S(2)}) collective-permute-start(f32[6,3,32,256]{3,2,1,0:T(8,128)} %collective-permute-done.1.refs_0_), channel_id=1, source_target_pairs={{0,64},{1,65},{2,66},{3,67},{4,68},{5,69},{6,70},{7,71},{8,72},{9,... | collective-permute-start | bytes 1769480 | tf_op jit(solution)/shard_map/ppermute | solution.py:249
  265.5 2.7 collective-permute-start.6
  268.2 1.8 collective-permute-start.7
  270.0 18.5 %collective-permute-start.8 = (f32[6,3,32,256]{3,2,1,0:T(8,128)}, f32[6,3,32,256]{3,2,1,0:T(8,128)}, u32[]{:S(2)}, u32[]{:S(2)}) collective-permute-start(f32[6,3,32,256]{3,2,1,0:T(8,128)} %collective-permute-done.1.refs_0_), channel_id=1, source_target_pairs={{0,112},{1,113},{2,114},{3,115},{4,116},{5,117},{6,118},{7,119},{8... | collective-permute-start | bytes 1769480 | tf_op jit(solution)/shard_map/ppermute | solution.py:249
  288.5 0.9 maximum_dynamic-update-slice_fusion.2
  289.4 0.9 maximum_dynamic-update-slice_fusion.1
  290.4 1.3 bitcast_add_fusion.4
  291.7 1.0 maximum_dynamic-update-slice_fusion.refs_13_
  292.6 71.0 %top.1 = (bf16[6,6,256,256]{3,2,1,0:T(8,128)(2,1)}, bf16[6,6,256,256]{3,2,1,0:T(8,128)(2,1)}, bf16[6,256,256]{2,1,0:T(8,128)(2,1)}, bf16[6,256,256]{2,1,0:T(8,128)(2,1)}, f32[6,256,256]{2,1,0:T(8,128)}) custom-call(f32[16,21,16,256]{3,2,1,0:T(8,128)} %bitcast.293), custom_call_target="tpu_custom_call" | custom-call | tf_op jit(solution)/shard_map/top/pallas_call | solution.py:126
  363.7 44.9 %finish.1 = f32[1536,768]{1,0:T(8,128)} custom-call(s32[2]{0:T(128)} %pad_add_fusion.place_ref, f32[16,6,6,16,256]{4,3,2,1,0:T(8,128)} %bitcast.291, f32[6,3,32,256]{3,2,1,0:T(8,128)} %collective-permute-done.1.refs_0_, f32[6,3,32,256]{3,2,1,0:T(8,128)} %copy-done.9, f32[6,3,32,256]{3,2,1,0:T(8,128)} %copy-done.10, ...), custom_call_target="tpu_custom_call" | custom-call | tf_op jit(solution)/shard_map/finish/pallas_call | solution.py:219
  (76 shorter events, 5.5 us)
Async XLA Ops:
  22.1 7.8 %copy-start.12 = (s32[2,32]{1,0:T(2,128)S(1)}, s32[2,32]{1,0:T(2,128)}, u32[]{:S(2)}) copy-start(s32[2,32]{1,0:T(2,128)} %param.7) | copy-start | bytes 772
  22.1 8.0 %copy-start.11 = (f32[12288]{0:T(1024)S(1)}, f32[12288]{0:T(1024)}, u32[]{:S(2)}) copy-start(f32[12288]{0:T(1024)} %param.5) | copy-start | bytes 147460
  23.6 10.6 %collective-permute-start = (f32[4,256,256]{2,1,0:T(8,128)}, f32[4,256,256]{2,1,0:T(8,128)S(1)}, u32[]{:S(2)}, u32[]{:S(2)}) collective-permute-start(f32[4,256,256]{2,1,0:T(8,128)} %get-tuple-element.52), channel_id=1, source_target_pairs={{0,64},{1,65},{2,66},{3,67},{4,68},{5,69},{16,80},{17,81},{18,82},... | collective-permute-start | bytes 3145736 | tf_op jit(solution)/shard_map/ppermute | solution.py:249
  24.3 29.7 %collective-permute-start.16 = (f32[4,256,256]{2,1,0:T(8,128)}, f32[4,256,256]{2,1,0:T(8,128)S(1)}, u32[]{:S(2)}, u32[]{:S(2)}) collective-permute-start(f32[4,256,256]{2,1,0:T(8,128)} %get-tuple-element.52), channel_id=1, source_target_pairs={{6,70},{7,71},{8,72},{9,73},{10,74},{11,75},{12,76},{13,77},{14,78... | collective-permute-start | bytes 3145736 | tf_op jit(solution)/shard_map/ppermute | solution.py:249
  28.5 46.8 %collective-permute-start.17 = (f32[4,256,256]{2,1,0:T(8,128)}, f32[4,256,256]{2,1,0:T(8,128)S(1)}, u32[]{:S(2)}, u32[]{:S(2)}) collective-permute-start(f32[4,256,256]{2,1,0:T(8,128)} %get-tuple-element.51), channel_id=1, source_target_pairs={{0,64},{1,65},{2,66},{3,67},{4,68},{5,69},{6,70},{7,71},{8,72},{9,... | collective-permute-start | bytes 3145736 | tf_op jit(solution)/shard_map/ppermute | solution.py:249
  34.3 41.0 %copy-start.6 = (f32[4,256,256]{2,1,0:T(8,128)}, f32[4,256,256]{2,1,0:T(8,128)S(1)}, u32[]{:S(2)}) copy-start(f32[4,256,256]{2,1,0:T(8,128)S(1)} %collective-permute-done) | copy-start | bytes 3145732
  54.0 21.3 %copy-start.7 = (f32[4,256,256]{2,1,0:T(8,128)}, f32[4,256,256]{2,1,0:T(8,128)S(1)}, u32[]{:S(2)}) copy-start(f32[4,256,256]{2,1,0:T(8,128)S(1)} %collective-permute-done.16) | copy-start | bytes 3145732
  75.3 1.0 copy-start.8
  80.3 1.0 copy-start.1
  80.3 2.9 copy-start.3
  83.2 13.6 %all-to-all-start = ((f32[16,16,256]{2,1,0:T(8,128)}), f32[16,16,256]{2,1,0:T(8,128)S(1)}, u32[]{:S(2)}, u32[]{:S(2)}) async-start(f32[16,16,256]{2,1,0:T(8,128)} %bitcast.13), calls=%async_computation | async-start | bytes 524288 | tf_op jit(solution)/shard_map/all_to_all | solution.py:309
  90.0 202.7 %all-gather.7.cloned.1.call-start = ((), (), s32[]{:S(2)}) async-start(), calls=%async_computation.3 | async-start | bytes 5849088 | tf_op jit(solution)/shard_map/all_gather | solution.py:318
  96.8 17.8 %collective-permute-start.9 = (f32[6,16,256]{2,1,0:T(8,128)S(1)}, f32[6,16,256]{2,1,0:T(8,128)S(1)}, u32[]{:S(2)}, u32[]{:S(2)}) collective-permute-start(f32[6,16,256]{2,1,0:T(8,128)S(1)} %get-tuple-element.53), channel_id=1, source_target_pairs={{0,16},{1,17},{2,18},{3,19},{4,20},{5,21},{6,22},{7,23},{8,24},{9,... | collective-permute-start | bytes 294920 | tf_op jit(solution)/shard_map/ppermute | solution.py:249
  99.2 16.7 %collective-permute-start.10 = (f32[6,16,256]{2,1,0:T(8,128)S(1)}, f32[6,16,256]{2,1,0:T(8,128)S(1)}, u32[]{:S(2)}, u32[]{:S(2)}) collective-permute-start(f32[6,16,256]{2,1,0:T(8,128)S(1)} %get-tuple-element.53), channel_id=1, source_target_pairs={{0,32},{1,33},{2,34},{3,35},{4,36},{5,37},{6,38},{7,39},{8,40},{9,... | collective-permute-start | bytes 294920 | tf_op jit(solution)/shard_map/ppermute | solution.py:249
  103.6 13.7 %collective-permute-start.11 = (f32[6,16,256]{2,1,0:T(8,128)S(1)}, f32[6,16,256]{2,1,0:T(8,128)S(1)}, u32[]{:S(2)}, u32[]{:S(2)}) collective-permute-start(f32[6,16,256]{2,1,0:T(8,128)S(1)} %get-tuple-element.53), channel_id=1, source_target_pairs={{0,48},{1,49},{2,50},{3,51},{4,52},{5,53},{6,54},{7,55},{8,56},{9,... | collective-permute-start | bytes 294920 | tf_op jit(solution)/shard_map/ppermute | solution.py:249
  106.0 11.3 %collective-permute-start.12 = (f32[6,16,256]{2,1,0:T(8,128)S(1)}, f32[6,16,256]{2,1,0:T(8,128)S(1)}, u32[]{:S(2)}, u32[]{:S(2)}) collective-permute-start(f32[6,16,256]{2,1,0:T(8,128)S(1)} %get-tuple-element.53), channel_id=1, source_target_pairs={{0,64},{1,65},{2,66},{3,67},{4,68},{5,69},{6,70},{7,71},{8,72},{9,... | collective-permute-start | bytes 294920 | tf_op jit(solution)/shard_map/ppermute | solution.py:249
  108.0 10.2 %collective-permute-start.13 = (f32[6,16,256]{2,1,0:T(8,128)S(1)}, f32[6,16,256]{2,1,0:T(8,128)S(1)}, u32[]{:S(2)}, u32[]{:S(2)}) collective-permute-start(f32[6,16,256]{2,1,0:T(8,128)S(1)} %get-tuple-element.53), channel_id=1, source_target_pairs={{0,80},{1,81},{2,82},{3,83},{4,84},{5,85},{6,86},{7,87},{8,88},{9,... | collective-permute-start | bytes 294920 | tf_op jit(solution)/shard_map/ppermute | solution.py:249
  114.6 3.5 collective-permute-start.14
  115.9 3.5 collective-permute-start.15
  123.2 240.5 %all-gather.5.cloned.1.call-start = ((), (), s32[]{:S(2)}) async-start(), calls=%async_computation.2 | async-start | bytes 10027008 | tf_op jit(solution)/shard_map/all_gather | solution.py:330
  132.0 4.2 %copy-start.2 = (f32[4,256,256]{2,1,0:T(8,128)S(1)}, f32[4,256,256]{2,1,0:T(8,128)}, u32[]{:S(2)}) copy-start(f32[4,256,256]{2,1,0:T(8,128)} %copy-done.1) | copy-start | bytes 3145732
  132.0 4.2 %copy-start.4 = (f32[4,256,256]{2,1,0:T(8,128)S(1)}, f32[4,256,256]{2,1,0:T(8,128)}, u32[]{:S(2)}) copy-start(f32[4,256,256]{2,1,0:T(8,128)} %copy-done.3) | copy-start | bytes 3145732
  198.4 1.6 copy-start.5
  204.5 1.9 copy-start
  215.4 11.3 %collective-permute-start.1 = (f32[6,3,32,256]{3,2,1,0:T(8,128)S(1)}, f32[6,3,32,256]{3,2,1,0:T(8,128)}, u32[]{:S(2)}, u32[]{:S(2)}) collective-permute-start(f32[6,3,32,256]{3,2,1,0:T(8,128)S(1)} %bitcast.302), channel_id=1, source_target_pairs={{0,0},{8,8},{1,16},{9,24},{2,32},{10,40},{3,48},{11,56},{4,64},{12... | collective-permute-start | bytes 1769480 | tf_op jit(solution)/shard_map/ppermute | solution.py:249
  226.7 41.5 %collective-permute-start.2 = (f32[6,3,32,256]{3,2,1,0:T(8,128)}, f32[6,3,32,256]{3,2,1,0:T(8,128)S(1)}, u32[]{:S(2)}, u32[]{:S(2)}) collective-permute-start(f32[6,3,32,256]{3,2,1,0:T(8,128)} %collective-permute-done.1.refs_0_), channel_id=1, source_target_pairs={{0,16},{1,17},{2,18},{3,19},{4,20},{5,21},{6,22},{7,23},{8,24},{9,... | collective-permute-start | bytes 1769480 | tf_op jit(solution)/shard_map/ppermute | solution.py:249
  226.7 43.3 %collective-permute-start.3 = (f32[6,3,32,256]{3,2,1,0:T(8,128)}, f32[6,3,32,256]{3,2,1,0:T(8,128)S(1)}, u32[]{:S(2)}, u32[]{:S(2)}) collective-permute-start(f32[6,3,32,256]{3,2,1,0:T(8,128)} %collective-permute-done.1.refs_0_), channel_id=1, source_target_pairs={{0,32},{1,33},{2,34},{3,35},{4,36},{5,37},{6,38},{7,39},{8,40},{9,... | collective-permute-start | bytes 1769480 | tf_op jit(solution)/shard_map/ppermute | solution.py:249
  248.2 115.4 %collective-permute-start.4 = (f32[6,3,32,256]{3,2,1,0:T(8,128)}, f32[6,3,32,256]{3,2,1,0:T(8,128)}, u32[]{:S(2)}, u32[]{:S(2)}) collective-permute-start(f32[6,3,32,256]{3,2,1,0:T(8,128)} %collective-permute-done.1.refs_0_), channel_id=1, source_target_pairs={{0,48},{1,49},{2,50},{3,51},{4,52},{5,53},{6,54},{7,55},{8,56},{9,... | collective-permute-start | bytes 1769480 | tf_op jit(solution)/shard_map/ppermute | solution.py:249
  248.8 114.8 %collective-permute-start.5 = (f32[6,3,32,256]{3,2,1,0:T(8,128)}, f32[6,3,32,256]{3,2,1,0:T(8,128)}, u32[]{:S(2)}, u32[]{:S(2)}) collective-permute-start(f32[6,3,32,256]{3,2,1,0:T(8,128)} %collective-permute-done.1.refs_0_), channel_id=1, source_target_pairs={{0,64},{1,65},{2,66},{3,67},{4,68},{5,69},{6,70},{7,71},{8,72},{9,... | collective-permute-start | bytes 1769480 | tf_op jit(solution)/shard_map/ppermute | solution.py:249
  265.5 98.1 %collective-permute-start.6 = (f32[6,3,32,256]{3,2,1,0:T(8,128)}, f32[6,3,32,256]{3,2,1,0:T(8,128)}, u32[]{:S(2)}, u32[]{:S(2)}) collective-permute-start(f32[6,3,32,256]{3,2,1,0:T(8,128)} %collective-permute-done.1.refs_0_), channel_id=1, source_target_pairs={{0,80},{1,81},{2,82},{3,83},{4,84},{5,85},{6,86},{7,87},{8,88},{9,... | collective-permute-start | bytes 1769480 | tf_op jit(solution)/shard_map/ppermute | solution.py:249
  268.2 23.5 %copy-start.9 = (f32[6,3,32,256]{3,2,1,0:T(8,128)}, f32[6,3,32,256]{3,2,1,0:T(8,128)S(1)}, u32[]{:S(2)}) copy-start(f32[6,3,32,256]{3,2,1,0:T(8,128)S(1)} %collective-permute-done.2.refs_1_) | copy-start | bytes 1769476
  268.2 95.5 %collective-permute-start.7 = (f32[6,3,32,256]{3,2,1,0:T(8,128)}, f32[6,3,32,256]{3,2,1,0:T(8,128)}, u32[]{:S(2)}, u32[]{:S(2)}) collective-permute-start(f32[6,3,32,256]{3,2,1,0:T(8,128)} %collective-permute-done.1.refs_0_), channel_id=1, source_target_pairs={{0,96},{1,97},{2,98},{3,99},{4,100},{5,101},{6,102},{7,103},{8,104... | collective-permute-start | bytes 1769480 | tf_op jit(solution)/shard_map/ppermute | solution.py:249
  270.0 21.7 %copy-start.10 = (f32[6,3,32,256]{3,2,1,0:T(8,128)}, f32[6,3,32,256]{3,2,1,0:T(8,128)S(1)}, u32[]{:S(2)}) copy-start(f32[6,3,32,256]{3,2,1,0:T(8,128)S(1)} %collective-permute-done.3.refs_2_) | copy-start | bytes 1769476
  270.0 93.6 %collective-permute-start.8 = (f32[6,3,32,256]{3,2,1,0:T(8,128)}, f32[6,3,32,256]{3,2,1,0:T(8,128)}, u32[]{:S(2)}, u32[]{:S(2)}) collective-permute-start(f32[6,3,32,256]{3,2,1,0:T(8,128)} %collective-permute-done.1.refs_0_), channel_id=1, source_target_pairs={{0,112},{1,113},{2,114},{3,115},{4,116},{5,117},{6,118},{7,119},{8... | collective-permute-start | bytes 1769480 | tf_op jit(solution)/shard_map/ppermute | solution.py:249
Sparse Core Ops, SparseCore 0:
  123.3 75.4 all-gather.6
  201.0 120.6 all-gather.4

commit v2 on v1

v2 whole, which is shorter than its diff:
```python
import jax
import jax.numpy as jnp
from jax import lax
from jax.experimental import pallas as pl
from jax.experimental.pallas import tpu as pltpu
from jax.sharding import PartitionSpec as P

PANELS = 6
BS=256
NT = (((1,), (1,)), ((), ()))
NN = (((1,), (0,)), ((), ()))

def split(x):
    hi = x.astype(jnp.bfloat16)
    return hi, (x - hi.astype(jnp.float32)).astype(jnp.bfloat16)

def dot(a, b, dims=NT):
    return lax.dot_general(a, b, dims, preferred_element_type=jnp.float32)

def dot3(ah, al, bh, bl, dims=NT):
    return dot(ah, bh, dims) + (dot(ah, bl, dims) + dot(al, bh, dims))

def mul3(a, b, dims=NT):
    return dot3(*split(a), *split(b), dims)

def leaf(sym):
    n = sym.shape[0]
    groups = n // 8
    lane = lax.broadcasted_iota(jnp.int32, (8, n), 1)
    sub = lax.broadcasted_iota(jnp.int32, (8, n), 0)
    across = lambda v, j: jnp.broadcast_to(v[:, j:j + 1], (8, n))
    down = lambda v, s: jnp.broadcast_to(v[s:s + 1, :], (8, n))
    rows = [sym[8 * h:8 * h + 8] for h in range(groups)]
    right = [jnp.where(lane == sub + 8 * h, 1.0, 0.0) for h in range(groups)]
    upper, inverse = [], []
    for g in range(groups):
        cols = [across(rows[g], 8 * g + t) for t in range(8)]
        a = {(s, t): down(cols[t], s) for t in range(8) for s in range(t, 8)}
        u = [down(rows[g], t) for t in range(8)]
        w = [down(right[g], t) for t in range(8)]
        later = range(g + 1, groups)
        x = {h: [across(rows[h], 8 * g + t) for t in range(8)] for h in later}
        for t in range(8):
            r = lax.rsqrt(a[t, t])
            for s in range(t + 1, 8):
                a[s, t] = a[s, t] * r
            u[t] = u[t] * r
            w[t] = w[t] * r
            for h in later:
                x[h][t] = x[h][t] * r
            for s in range(t + 1, 8):
                for v in range(t + 1, s + 1):
                    a[s, v] = a[s, v] - a[s, t] * a[v, t]
                u[s] = u[s] - a[s, t] * u[t]
                w[s] = w[s] - a[s, t] * w[t]
                for h in later:
                    x[h][s] = x[h][s] - a[s, t] * x[h][t]
        for h in later:
            for t in range(8):
                rows[h] = rows[h] - x[h][t] * u[t]
                right[h] = right[h] - x[h][t] * w[t]
        ug, wg = u[0], w[0]
        for t in range(1, 8):
            ug = jnp.where(sub == t, u[t], ug)
            wg = jnp.where(sub == t, w[t], wg)
        upper.append(jnp.where(lane >= sub + 8 * g, ug, 0.0))
        inverse.append(wg)
    return jnp.concatenate(upper, axis=0).T, jnp.concatenate(inverse, axis=0)

def symmetric(d):
    n = d.shape[0]
    below = lax.broadcasted_iota(jnp.int32, (n, n), 0) >= lax.broadcasted_iota(jnp.int32, (n, n), 1)
    return jnp.where(below, d, d.T)

LEAF = 128


def top_kernel(first, last, in_ref, *refs):
    lows, refs = refs[:2 * (min(last, PANELS - 1) - first)], refs[2 * (min(last, PANELS - 1) - first):]
    ih_ref, il_ref, fac_ref, refs = refs[0], refs[1], refs[2], refs[3:]
    if last < PANELS:
        on_ref, refs = refs[0], refs[1:]
    a_ref, s_ref, f_ref, w_ref = refs
    if first == 0:
        e = 0
        for i in range(PANELS):
            for k in range(i + 1):
                a_ref[k * PANELS + i] = in_ref[:, e].reshape(BS, BS)
                e += 1
    else:
        e = 0
        for k in range(first, PANELS):
            a_ref[k * PANELS + k:(k + 1) * PANELS] = in_ref[e:e + PANELS - k]
            e += PANELS - k
    zero = jnp.zeros((LEAF, LEAF), jnp.float32)

    def panel(k, carry):
        d = a_ref[k * PANELS + k]
        s_ref[0] = d[:LEAF, :LEAF]
        s_ref[1] = d[LEAF:, LEAF:]
        s_ref[2] = d[LEAF:, :LEAF]

        def half(h, carry):
            factor, inverse = leaf(symmetric(s_ref[h]))
            f_ref[h] = factor
            w_ref[h] = inverse

            @pl.when(h == 0)
            def _():
                low = mul3(s_ref[2], inverse)
                s_ref[2] = low
                s_ref[1] = s_ref[1] - mul3(low, low)
            return carry
        lax.fori_loop(0, 2, half, 0)
        corner = -mul3(w_ref[1], mul3(s_ref[2], w_ref[0], NN), NN)
        fac_ref[k - first] = jnp.concatenate(
            [jnp.concatenate([f_ref[0], zero], 1), jnp.concatenate([s_ref[2], f_ref[1]], 1)], 0
        )
        inv = jnp.concatenate([jnp.concatenate([w_ref[0], zero], 1), jnp.concatenate([corner, w_ref[1]], 1)], 0)
        ih, il = split(inv)
        ih_ref[k - first] = ih
        il_ref[k - first] = il
        for at in range(first, min(last, PANELS - 1)):
            @pl.when(k == at)
            def _(at=at):
                rest = PANELS - 1 - at
                below = a_ref[at * PANELS + at + 1:(at + 1) * PANELS].reshape(rest * BS, BS)
                xh, xl = split(dot3(*split(below), ih, il))
                lows[2 * (at - first)][...] = xh.reshape(rest, BS, BS)
                lows[2 * (at - first) + 1][...] = xl.reshape(rest, BS, BS)
                for j in range(at + 1, PANELS):
                    o = (j - at - 1) * BS
                    old = a_ref[j * PANELS + j:(j + 1) * PANELS]
                    upd = dot3(xh[o:], xl[o:], xh[o:o + BS], xl[o:o + BS])
                    a_ref[j * PANELS + j:(j + 1) * PANELS] = old - upd.reshape(PANELS - j, BS, BS)
        return carry
    lax.fori_loop(first, last, panel, 0)
    if last < PANELS:
        e = 0
        for k in range(last, PANELS):
            on_ref[e:e + PANELS - k] = a_ref[k * PANELS + k:(k + 1) * PANELS]
            e += PANELS - k


def top_part(first, last, blocks):
    f32, bf = jnp.float32, jnp.bfloat16
    n = last - first
    shapes = []
    for at in range(first, min(last, PANELS - 1)):
        shapes += [jax.ShapeDtypeStruct((PANELS - 1 - at, BS, BS), bf)] * 2
    low_count = len(shapes)
    shapes += [jax.ShapeDtypeStruct((n, BS, BS), bf)] * 2 + [jax.ShapeDtypeStruct((n, BS, BS), f32)]
    left = PANELS - last
    if left:
        shapes.append(jax.ShapeDtypeStruct((left * (left + 1) // 2, BS, BS), f32))
    out = pl.pallas_call(
        lambda *refs: top_kernel(first, last, *refs),
        out_shape=shapes,
        scratch_shapes=[
            pltpu.VMEM((PANELS * PANELS, BS, BS), f32),
            pltpu.VMEM((3, LEAF, LEAF), f32),
            pltpu.VMEM((2, LEAF, LEAF), f32),
            pltpu.VMEM((2, LEAF, LEAF), f32),
        ],
        compiler_params=pltpu.CompilerParams(vmem_limit_bytes=40 * 2**20),
        cost_estimate=pl.CostEstimate(flops=n * 11 * 10**9, bytes_accessed=n * 40 * 10**6, transcendentals=n * BS),
        name="top" + str(first),
    )(blocks)
    return out[:low_count], out[low_count:low_count + 3], out[-1] if left else None

HALF_ROWS = 4
N_ROW = 8
N_COL = 16
STRIP = BS // N_COL
ROW_SLOTS = 6
COL_SLOTS = 3
CHILD_SLOTS = 4
ROW_TILE = 2


CUTS = (0, 2, 4, 6)
LOWS = PANELS - 1
PARTS = len(CUTS) - 1


def part_of(k):
    i = max(j for j in range(PARTS) if CUTS[j] <= k)
    return i, k - CUTS[i]


def solve_rows(x_ref, f_ref, h_ref, l_ref, rows, lows, invs):
    for k in range(PANELS):
        acc = x_ref[k, :rows]
        for m in range(k):
            acc = acc - dot3(h_ref[m], l_ref[m], lows[2 * m][k - m - 1], lows[2 * m + 1][k - m - 1])
        i, o = part_of(k)
        out = dot3(*split(acc), invs[3 * i][o], invs[3 * i + 1][o])
        hi, lo = split(out)
        h_ref[k] = hi
        l_ref[k] = lo
        if f_ref is not None:
            f_ref[k] = out


def rows_kernel(place_ref, row_at_ref, col_at_ref, row_ref, *refs):
    piece_ref, refs = refs[0], refs[1:]
    lows, refs = refs[:2 * LOWS], refs[2 * LOWS:]
    invs, refs = refs[:3 * PARTS], refs[3 * PARTS:]
    shift_ref, child_ref, near_ref, rest_ref, late_ref, tail_ref, front_ref, out_ref = refs[:8]
    x_ref, f_ref, rh_ref, rl_ref, ch_ref, cl_ref = refs[8:]
    r, c = place_ref[0], place_ref[1]
    side = r // HALF_ROWS
    step = pl.program_id(0)
    blank = jnp.zeros((BS, BS), jnp.bfloat16)

    @pl.when(step == 0)
    def _():
        part = BS // N_ROW
        for i in range(N_ROW):
            x, y = (i + c) % HALF_ROWS, (i // HALF_ROWS) ^ side
            for k in range(PANELS):
                for s in range(COL_SLOTS):
                    at = s * BS + i * part
                    x_ref[k, at:at + part] = piece_ref[x, y, k, s]
        solve_rows(x_ref, None, ch_ref, cl_ref, COL_SLOTS * BS, lows, invs)
        for k in range(PANELS):
            @pl.when(k >= c)
            def _(k=k):
                ch_ref[k, :BS] = blank
                cl_ref[k, :BS] = blank

    @pl.when(step > 0)
    def _():
        rows = ROW_TILE * BS
        for k in range(PANELS):
            for s in range(ROW_TILE):
                x_ref[k, s * BS:(s + 1) * BS] = row_ref[:, k, s].reshape(BS, BS)
        solve_rows(x_ref, f_ref, rh_ref, rl_ref, rows, lows, invs)

        @pl.when(step == 1)
        def _():
            for k in range(PANELS):
                @pl.when(k >= r)
                def _(k=k):
                    rh_ref[k, :BS] = blank
                    rl_ref[k, :BS] = blank
        acc = front_ref[...]
        for k in range(PANELS):
            acc = acc - dot3(rh_ref[k], rl_ref[k], ch_ref[k], cl_ref[k])
        out_ref[...] = acc

        eye = lax.broadcasted_iota(jnp.int32, (BS, BS), 0) == lax.broadcasted_iota(jnp.int32, (BS, BS), 1)
        for s in range(ROW_TILE):
            p = (step - 1) * ROW_TILE + s
            here = slice(s * BS, (s + 1) * BS)
            for t in range(COL_SLOTS):
                there = slice(t * BS, (t + 1) * BS)

                @pl.when(p * N_ROW + r == t * N_COL + c)
                def _(p=p, here=here, there=there):
                    out_ref[here, there] += jnp.where(eye, shift_ref[pl.ds(p * N_ROW + r, 1), :], 0.0)
                for h in range(2):
                    for q in (s, s + 2):
                        for u in (0, 1):
                            if not 0 <= t - u <= 1:
                                continue
                            hit = (row_at_ref[h * CHILD_SLOTS + q] == p) & (col_at_ref[h * 2 + u] == t)

                            @pl.when(hit & (side == h))
                            def _(here=here, there=there, q=q, u=u):
                                out_ref[here, there] += child_ref[q, side, :, u * BS:(u + 1) * BS]

                            @pl.when(hit & (side != h))
                            def _(here=here, there=there, q=q, u=u):
                                if u == 1:
                                    arrived = tail_ref[q]
                                else:
                                    arrived = late_ref[q] + (near_ref[0] if q == 0 else rest_ref[q - 1])
                                out_ref[here, there] += arrived
            level = p * N_ROW + r

            @pl.when((c < PANELS) & (level > c))
            def _(here=here):
                out_ref[here, :BS] = f_ref[c, here]

            for k in range(PANELS):
                @pl.when((c == k) & (level == k))
                def _(here=here, k=k):
                    i, o = part_of(k)
                    out_ref[here, :BS] = invs[3 * i + 2][o]


def finish(place, row_at, col_at, row_panel, col_panel, lows, invs, shift, child, near, rest, late, tail, front):
    f32, bf = jnp.float32, jnp.bfloat16
    tiles = ROW_SLOTS // ROW_TILE
    whole = pl.BlockSpec(memory_space=pltpu.VMEM)
    smem = pl.BlockSpec(memory_space=pltpu.SMEM)
    tile_at = lambda g: jnp.maximum(g - 1, 0)
    rows, cols = ROW_TILE * BS, COL_SLOTS * BS
    front_spec = pl.BlockSpec((rows, cols), lambda g: (tile_at(g), 0))
    return pl.pallas_call(
        rows_kernel,
        grid=(tiles + 1,),
        in_specs=[smem] * 3
        + [pl.BlockSpec((N_COL, PANELS, ROW_TILE, STRIP, BS), lambda g: (0, 0, tile_at(g), 0, 0))]
        + [whole] * (1 + 2 * LOWS + 3 * PARTS + 6)
        + [front_spec],
        out_specs=front_spec,
        out_shape=jax.ShapeDtypeStruct(front.shape, f32),
        scratch_shapes=[
            pltpu.VMEM((PANELS, cols, BS), f32),
            pltpu.VMEM((PANELS, rows, BS), f32),
            pltpu.VMEM((PANELS, rows, BS), bf),
            pltpu.VMEM((PANELS, rows, BS), bf),
            pltpu.VMEM((PANELS, cols, BS), bf),
            pltpu.VMEM((PANELS, cols, BS), bf),
        ],
        compiler_params=pltpu.CompilerParams(vmem_limit_bytes=60 * 2**20),
        name="finish",
    )(place, row_at, col_at, row_panel, col_panel, *lows, *invs, shift, child, near, rest, late, tail, front)


def device(r, c):
    return r * N_COL + c


def permute(x, pairs):
    return lax.ppermute(x, ("row", "col"), pairs)


def swap_rows(x, apart, cols):
    return permute(x, [(device(r, c), device(r ^ apart, c)) for r in range(N_ROW) for c in cols])


def after(x, *others):
    return lax.optimization_barrier((x, *others))[0]


def on_device(front_orig, pivot_shift, child_update, child_map):
    r = lax.axis_index("row")
    c = lax.axis_index("col")
    first = r < HALF_ROWS

    child = child_update.reshape(CHILD_SLOTS, 2, BS, 2 * BS)

    def leaving(cols):
        return jnp.where(first, child[:, 1, :, cols], child[:, 0, :, cols])

    lead = leaving(slice(0, BS))
    near_in = swap_rows(lead[:1], HALF_ROWS, range(PANELS))
    entry = jnp.arange(child_map.shape[1], dtype=jnp.int32)
    want_row = jnp.arange(CHILD_SLOTS, dtype=jnp.int32) * N_ROW + r
    want_col = jnp.arange(2, dtype=jnp.int32) * N_COL + c

    def lookup(wanted):
        hit = wanted[None, :, None] == entry[None, None, :]
        return jnp.sum(jnp.where(hit, child_map[:, None, :], 0), axis=2)

    row_at = lookup(want_row) // N_ROW
    col_at = lookup(want_col) // N_COL

    staying = jnp.where(first, child[:, 0, :, :BS], child[:, 1, :, :BS])
    own = lax.dynamic_index_in_dim(pivot_shift.reshape(ROW_SLOTS, N_ROW, BS), r, axis=1, keepdims=False)
    eye = lax.broadcasted_iota(jnp.int32, (BS, BS), 0) == lax.broadcasted_iota(jnp.int32, (BS, BS), 1)

    def raw_tile(p):
        tile = front_orig[p * BS:(p + 1) * BS, :BS]
        if p == 0:
            tile = tile + jnp.where(eye & (r == c), own[0][:, None], 0.0)
        for h in range(2):
            for q in range(p % 2, CHILD_SLOTS, 2):
                if 0 <= p - q <= 2:
                    arrived = near_in[0] if q == 0 else rest_in[q - 1]
                    part = jnp.where(first == (h == 0), staying[q], arrived)
                    hit = (col_at[h, 0] == 0) & (row_at[h, q] == p)
                    tile = tile + jnp.where(hit, part, 0.0)
        return tile.reshape(N_COL, STRIP, BS)

    def row_gather(x, *groups):
        n = len(groups[0])
        groups = None if n == N_ROW else [list(g) for g in groups]
        return lax.all_to_all(jnp.broadcast_to(x, (n, *x.shape)), "row", 0, 0, axis_index_groups=groups)

    strips = lax.all_to_all(raw_tile(0), "col", 0, 0)[:PANELS]
    rest_in = swap_rows(after(lead[1:], strips), HALF_ROWS, range(PANELS))
    near = row_gather(strips, range(N_ROW))
    packed = jnp.concatenate([near[i, : i + 1] for i in range(PANELS)], axis=0)
    top = lax.all_gather(packed, "col")

    column = jnp.stack([raw_tile(p) for p in range(1, ROW_SLOTS)], axis=1)
    dealt = lax.all_to_all(after(column, packed), "col", 0, 0)[:PANELS]
    dealt = jnp.concatenate([strips[:, None], dealt], axis=1)

    lows0, invs0, blocks0 = top_part(CUTS[0], CUTS[1], top)
    lows1, invs1, blocks1 = top_part(CUTS[1], CUTS[2], blocks0)
    lows2, invs2, _ = top_part(CUTS[2], CUTS[3], blocks1)
    lows, invs = lows0 + lows1 + lows2, invs0 + invs1 + invs2

    even, odd = dealt[:, 0::2], dealt[:, 1::2]
    is_odd = c % 2 == 1
    upper = c >= N_ROW

    def turned(flip, far):
        pairs = []
        for i in range(N_ROW):
            for j in range(N_COL):
                to = (j // N_ROW) ^ far
                to = to * HALF_ROWS + (i + j % N_ROW // 2) % HALF_ROWS
                pairs.append((device(i, j), device(to, (j % 2 ^ flip) * N_ROW + i)))
        return permute(jnp.where(is_odd != (flip == 1), odd, even), pairs)

    pair = []
    for far in (0, 1):
        straight, crossed = after(turned(0, far), blocks0), after(turned(1, far), blocks0)
        pair.append(
            jnp.concatenate([jnp.where(upper, crossed, straight), jnp.where(upper, straight, crossed)], axis=2)
        )
    pair = jnp.stack(pair)
    col_panel = row_gather(pair, range(HALF_ROWS), range(HALF_ROWS, N_ROW))

    row_panel = lax.all_gather(after(dealt, top), "col")

    lead_late = swap_rows(after(lead, blocks0), HALF_ROWS, range(PANELS, N_COL))
    tail_in = swap_rows(after(leaving(slice(BS, 2 * BS)), blocks0), HALF_ROWS, range(N_COL))

    place = jnp.stack([r, c]).astype(jnp.int32)
    return finish(
        place, row_at.reshape(-1), col_at.reshape(-1), row_panel, col_panel, lows, invs,
        pivot_shift.reshape(-1, BS), child, near_in, rest_in, lead_late, tail_in, front_orig,
    )


def solution(mesh):
    in_specs = (P("row", "col"), P(), P("row", "col"), P())
    out_specs = P("row", "col")
    return jax.shard_map(
        on_device, mesh=mesh, in_specs=in_specs, out_specs=out_specs, check_vma=False
    )
```

time: 423 us -> 297 us (0.70); the launches traced: 415 us -> 294 us
  starting transfers between devices: 94.1 us -> 30.3 us
  waiting for transfers between devices: 55.7 us -> 12.1 us
  blocking collectives: 55 us -> 85.1 us
  other arithmetic: 41.4 us -> 14.5 us
  local copies, waits for them, and re-layouts: 24.6 us -> 14.6 us
  Pallas kernels: 116 us -> 111 us
    ppermute x18 -> x8, starting transfers between devices: 87.3 us -> 23.8 us  [permute(): return lax.ppermute(x, ('row', 'col'), pairs)]
    ppermute x18 -> x8, waiting for transfers between devices: 48.9 us -> 12 us  [permute(): return lax.ppermute(x, ('row', 'col'), pairs)]
    all_to_all x1 -> x3, blocking collectives: 55 us -> 85.1 us  [the longest x1 48.1 us: on_device(): dealt = lax.all_to_all(after(column, packed), 'col', 0, 0)[:PANELS]]
    unnamed x10 -> x0, other arithmetic: 14.3 us -> none
    add x13 -> x5, other arithmetic: 14 us -> 4.88 us  [the longest x4 4.87 us: raw_tile(): tile = tile + jnp.where(hit, part, 0.0)]
    slice x7 -> x6, local copies, waits for them, and re-layouts: 8.13 us -> 1.34 us  [the longest x2 1.23 us: raw_tile(): hit = (col_at[h, 0] == 0) & (row_at[h, q] == p)]
    reshape x2 -> x1, local copies, waits for them, and re-layouts: 7.42 us -> 0.63 us  [on_device(): pivot_shift.reshape(-1, BS)]
    all_to_all x1, waiting for transfers between devices: 6.72 us -> 0.01 us  [row_gather(): lax.all_to_all(jnp.broadcast_to(x, (n, *x.shape)), 'row', 0, 0, axis_inde...]
  transfers between devices with their start and end apart: 21 -> 11, of which waited for: 6 -> 1; matrix products, arithmetic and copies ran while one was open for 9% -> 5% of each run, Pallas kernels for 17% -> 22%
where the time goes in v2:
time: 297 us; the launch traced here: 294 us
  Pallas kernels  111 us (37%)
  blocking collectives  85.1 us (29%)
  starting transfers between devices  30.3 us (10%)
  between operations  25.8 us (9%)
  local copies, waits for them, and re-layouts  14.6 us (5%)
  other arithmetic  14.5 us (5%)
  waiting for transfers between devices  12.1 us (4%)
    pallas_call x3, Pallas kernels, top_part(): pl.pallas_call(lambda *refs: top_kernel(first, last, *refs), out_shape=sh...  64.3 us
    all_to_all x1, blocking collectives, on_device(): dealt = lax.all_to_all(after(column, packed), 'col', 0, 0)[:PANELS]  48.1 us
    pallas_call x1, Pallas kernels, finish(): pl.pallas_call(rows_kernel, grid=(tiles + 1,), in_specs=[smem] * 3 + [pl....  47.2 us
    ppermute x8, starting transfers between devices, permute(): return lax.ppermute(x, ('row', 'col'), pairs)  23.8 us
    all_to_all x1, blocking collectives, row_gather(): lax.all_to_all(jnp.broadcast_to(x, (n, *x.shape)), 'row', 0, 0, axis_inde...  20 us
    all_to_all x1, blocking collectives, on_device(): strips = lax.all_to_all(raw_tile(0), 'col', 0, 0)[:PANELS]  16.9 us
    ppermute x8, waiting for transfers between devices, permute(): return lax.ppermute(x, ('row', 'col'), pairs)  12 us
    unnamed x63, local copies, waits for them, and re-layouts  9.49 us
  transfers between devices with their start and end apart: 11, of which 1 were waited for; matrix products, arithmetic and copies ran while one was open for 5% of the time, Pallas kernels for 22%

profile of v2, /device:TPU:10, one launch (start us, length us, event | category | flops | bytes accessed | tf_op | source)
XLA Modules:
  0.0 293.7 jit_solution(6018263063936044108)
XLA Ops:
  6.5 3.6 %fusion.1 = (f32[4,256,256]{2,1,0:T(8,128)}, f32[4,1,256,256]{3,2,0,1:T(8,128)S(1)}) fusion(f32[4,2,256,512]{3,2,1,0:T(8,128)} %bitcast.201, pred[]{:T(512)S(6)} %lt.14), kind=kLoop, calls=%fused_computation.3 | loop fusion | flops 524288 | bytes 6291457 | tf_op jit(solution)/shard_map/jit(_where)/select_n | solution.py:347
  10.1 0.7 collective-permute-start
  10.8 0.1 iota_compare_fusion.1
  10.9 0.1 select_reduce_fusion
  11.1 0.7 fusion.16
  11.8 0.1 iota_compare_fusion.2
  11.8 0.1 select_reduce_fusion.1
  12.0 0.5 fusion.17
  15.2 1.7 bitcast_select_fusion.1
  16.9 0.0 collective-permute-done.refs_22_
  16.9 1.2 bitcast_add_fusion.14
  18.1 16.9 %all_to_all.20 = f32[16,16,256]{2,1,0:T(8,128)S(1)} all-to-all(f32[16,16,256]{2,1,0:T(8,128)S(1)} %bitcast.210), channel_id=1, replica_groups=mesh['row'=8,'col'=16] {'col'}, dimensions={0} | all-to-all | bytes 524288 | tf_op jit(solution)/shard_map/all_to_all | solution.py:384
  34.9 0.1 broadcast_in_dim.99
  35.0 20.0 %all_to_all.21 = f32[8,6,16,256]{3,2,1,0:T(8,128)S(1)} all-to-all(f32[8,6,16,256]{3,2,1,0:T(8,128)S(1)} %broadcast_in_dim.99), channel_id=1, replica_groups=mesh['row'=8,'col'=16] {'row'}, dimensions={0} | all-to-all | bytes 1572864 | tf_op jit(solution)/shard_map/all_to_all | solution.py:382
  55.1 0.0 copy-start.24
  55.2 0.7 copy-done.24
  55.9 0.0 all-gather.5.cloned.1.call-update
  55.9 0.0 all-gather.7.cloned.1.call-start
  56.0 0.1 slice_bitcast_fusion.2
  56.0 0.7 collective-permute-start.1
  65.5 0.0 collective-permute-done.1.refs_23_
  65.5 1.6 bitcast_add_fusion
  67.2 1.1 bitcast_add_fusion.8
  68.3 1.1 bitcast_add_fusion.4
  69.4 48.1 %all_to_all.22 = f32[16,5,16,256]{3,2,1,0:T(8,128)S(1)} all-to-all(f32[16,5,16,256]{3,2,1,0:T(8,128)S(1)} %constant_dynamic-update-slice_fusion), channel_id=1, replica_groups=mesh['row'=8,'col'=16] {'col'}, dimensions={0} | all-to-all | bytes 2621440 | tf_op jit(solution)/shard_map/all_to_all | solution.py:391
  117.6 0.9 pad_maximum_fusion.1
  118.5 0.0 all-gather.7.cloned.1.call-update
  118.5 0.1 reduce_sum.23
  118.6 0.1 reduce_sum.25
  118.7 0.6 reshape.207.refs_20_
  119.3 0.6 pad_add_fusion.place_ref
  119.9 0.5 and_select_fusion.3.row_at_ref
  120.4 0.6 and_select_fusion.2.col_at_ref
  121.0 1.0 slice_select_fusion.1
  122.0 1.9 collective-permute-start.3
  123.9 3.3 %collective-permute-start.5 = (f32[6,3,16,256]{3,2,1,0:T(8,128)S(1)}, f32[6,3,16,256]{3,2,1,0:T(8,128)S(1)}, u32[]{:S(2)}, u32[]{:S(2)}) collective-permute-start(f32[6,3,16,256]{3,2,1,0:T(8,128)S(1)} %get-tuple-element.71), channel_id=1, source_target_pairs={{0,64},{1,72},{2,80},{3,88},{4,96},{5,104},{6,112},{7,120},{8,0},{... | collective-permute-start | bytes 884744 | tf_op jit(solution)/shard_map/ppermute | solution.py:328
  127.2 6.3 %collective-permute-start.2 = (f32[6,3,16,256]{3,2,1,0:T(8,128)S(1)}, f32[6,3,16,256]{3,2,1,0:T(8,128)S(1)}, u32[]{:S(2)}, u32[]{:S(2)}) collective-permute-start(f32[6,3,16,256]{3,2,1,0:T(8,128)S(1)} %get-tuple-element.70), channel_id=1, source_target_pairs={{0,8},{1,0},{2,24},{3,16},{4,40},{5,32},{6,56},{7,48},{8,72},{9,64... | collective-permute-start | bytes 884744 | tf_op jit(solution)/shard_map/ppermute | solution.py:328
  133.5 2.1 collective-permute-start.4
  135.6 2.6 copy-done.19
  138.2 24.2 %top0.1 = (bf16[5,256,256]{2,1,0:T(8,128)(2,1)S(1)}, bf16[5,256,256]{2,1,0:T(8,128)(2,1)S(1)}, bf16[4,256,256]{2,1,0:T(8,128)(2,1)S(1)}, bf16[4,256,256]{2,1,0:T...) custom-call(f32[16,21,16,256]{3,2,1,0:T(8,128)S(1)} %bitcast.200), custom_call_target="tpu_custom_call" | custom-call | flops 22000001024 | bytes 80000000 | tf_op jit(solution)/shard_map/top0/pallas_call | solution.py:156
  162.5 0.0 collective-permute-done.2
  162.5 0.1 broadcast_select_fusion.1
  162.7 0.5 copy-done
  163.2 0.2 copy-done.1
  163.5 0.2 copy-done.2
  163.6 0.2 copy-done.3
  163.8 0.2 copy-done.4
  164.0 0.2 copy-done.9
  164.2 0.1 copy-done.10
  164.3 0.1 pad_maximum_fusion
  164.4 2.8 broadcast_in_dim.100
  167.2 6.5 %all-to-all-start.3 = ((f32[4,2,6,3,32,256]{5,4,3,2,1,0:T(8,128)}), f32[4,2,6,3,32,256]{5,4,3,2,1,0:T(8,128)}, u32[]{:S(2)}, u32[]{:S(2)}) async-start(f32[4,2,6,3,32,256]{5,4,3,2,1,0:T(8,128)} %broadcast_in_dim.100), calls=%async_computation.3 | async-start | bytes 9437184 | tf_op jit(solution)/shard_map/all_to_all | solution.py:382
  173.7 8.6 %collective-permute-start.6 = (f32[4,256,256]{2,1,0:T(8,128)}, f32[4,256,256]{2,1,0:T(8,128)S(1)}, u32[]{:S(2)}, u32[]{:S(2)}) collective-permute-start(f32[4,256,256]{2,1,0:T(8,128)} %bitcast.206), channel_id=1, source_target_pairs={{6,70},{7,71},{8,72},{9,73},{10,74},{11,75},{12,76},{13,77},{14,78... | collective-permute-start | bytes 3145736 | tf_op jit(solution)/shard_map/ppermute | solution.py:328
  182.3 0.3 collective-permute-start.7
  182.6 20.9 %top2.1 = (bf16[3,256,256]{2,1,0:T(8,128)(2,1)S(1)}, bf16[3,256,256]{2,1,0:T(8,128)(2,1)S(1)}, bf16[2,256,256]{2,1,0:T(8,128)(2,1)S(1)}, bf16[2,256,256]{2,1,0:T...) custom-call(f32[10,256,256]{2,1,0:T(8,128)S(1)} %get-tuple-element.3, ...), custom_call_target="tpu_custom_call" | custom-call | flops 22000001024 | bytes 80000000 | tf_op jit(solution)/shard_map/top2/pallas_call | solution.py:156
  203.6 19.1 %top4.1 = (bf16[1,256,256]{2,1,0:T(8,128)(2,1)S(1)}, bf16[1,256,256]{2,1,0:T(8,128)(2,1)S(1)}, bf16[2,256,256]{2,1,0:T(8,128)(2,1)S(1)}, bf16[2,256,256]{2,1,0:T(8,128)(2,1)S(1)}, f32[2,256,256]{2,1,0:T(8,128)S(1)}) custom-call(f32[3,256,256]{2,1,0:T(8,128)S(1)} %get-tuple-element.51.refs_0_), custom_call_target="tpu_custom_call" | custom-call | flops 22000001024 | bytes 80000000 | tf_op jit(solution)/shard_map/top4/pallas_call | solution.py:156
  222.7 0.8 copy-done.6
  223.5 0.7 copy-done.15
  224.2 0.7 copy-done.16
  224.9 0.6 copy-done.17
  225.6 0.7 copy-done.18
  226.3 1.0 copy-done.23
  227.2 12.0 %collective-permute-done.7.refs_25_ = f32[4,256,256]{2,1,0:T(8,128)} collective-permute-done((f32[4,256,256]{2,1,0:T(8,128)}, f32[4,256,256]{2,1,0:T(8,128)}, u32[]{:S(2)}, u32[]{:S(2)}) %collective-permute-start.7) | collective-permute-done | bytes 1048608 | tf_op jit(solution)/shard_map/ppermute | solution.py:328
  239.2 47.2 %finish.1 = f32[1536,768]{1,0:T(8,128)} custom-call(s32[2]{0:T(128)} %pad_add_fusion.place_ref, s32[8]{0:T(128)} %and_select_fusion.3.row_at_ref, s32[4]{0:T(128)} %and_select_fusion.2.col_at_ref, f32[16,6,6,16,256]{4,3,2,1,0:T(8,128)} %bitcast.204, f32[4,2,6,3,32,256]{5,4,3,2,1,0:T(8,128)} %all-to-all-done.3.refs_0_, bf16[5,256,256]{2,1,0:T(8,128)(2,1)} %copy-done, ...), custom_call_target="tpu_custom_call" | custom-call | tf_op jit(solution)/shard_map/finish/pallas_call | solution.py:301
  (68 shorter events, 0.4 us)
Async XLA Ops:
  6.5 111.9 %all-gather.5.cloned.1.call-start = ((), (), s32[]{:S(2)}) async-start(), calls=%async_computation.4 | async-start | bytes 5849088 | tf_op jit(solution)/shard_map/all_gather | solution.py:388
  6.5 4.4 %copy-start.26 = (s32[2,32]{1,0:T(2,128)S(1)}, s32[2,32]{1,0:T(2,128)}, u32[]{:S(2)}) copy-start(s32[2,32]{1,0:T(2,128)} %param.7) | copy-start | bytes 772
  6.5 8.6 %copy-start.25 = (f32[12288]{0:T(1024)S(1)}, f32[12288]{0:T(1024)}, u32[]{:S(2)}) copy-start(f32[12288]{0:T(1024)} %param.5) | copy-start | bytes 147460
  10.1 45.8 %copy-start.21 = (f32[4,1,256,256]{3,2,0,1:T(8,128)}, f32[4,1,256,256]{3,2,0,1:T(8,128)S(1)}, u32[]{:S(2)}) copy-start(f32[4,1,256,256]{3,2,0,1:T(8,128)S(1)} %get-tuple-element.69) | copy-start | bytes 3145732
  10.1 6.7 %collective-permute-start = (f32[1,256,256]{2,1,0:T(8,128)S(1)}, f32[1,256,256]{2,1,0:T(8,128)S(1)}, u32[]{:S(2)}, u32[]{:S(2)}) collective-permute-start(f32[1,256,256]{2,1,0:T(8,128)S(1)} %slice_bitcast_fusion.6), channel_id=1, source_target_pairs={{0,64},{1,65},{2,66},{3,67},{4,68},{5,69},{16,80},{17,81},{18,82},... | collective-permute-start | bytes 786440 | tf_op jit(solution)/shard_map/ppermute | solution.py:328
  16.9 50.3 %copy-start.22 = (f32[1,256,256]{2,1,0:T(8,128)}, f32[1,256,256]{2,1,0:T(8,128)S(1)}, u32[]{:S(2)}) copy-start(f32[1,256,256]{2,1,0:T(8,128)S(1)} %collective-permute-done.refs_22_) | copy-start | bytes 786436
  55.1 0.7 copy-start.24
  55.9 183.3 %all-gather.7.cloned.1.call-start = ((), (), s32[]{:S(2)}) async-start(), calls=%async_computation.5 | async-start | bytes 10027008 | tf_op jit(solution)/shard_map/all_gather | solution.py:421
  56.0 9.5 %collective-permute-start.1 = (f32[3,256,256]{2,1,0:T(8,128)S(1)}, f32[3,256,256]{2,1,0:T(8,128)S(1)}, u32[]{:S(2)}, u32[]{:S(2)}) collective-permute-start(f32[3,256,256]{2,1,0:T(8,128)S(1)} %slice_bitcast_fusion.2), channel_id=1, source_target_pairs={{0,64},{1,65},{2,66},{3,67},{4,68},{5,69},{16,80},{17,81},{18,82},... | collective-permute-start | bytes 2359304 | tf_op jit(solution)/shard_map/ppermute | solution.py:328
  65.5 2.7 copy-start.20
  122.0 40.5 %collective-permute-start.3 = (f32[6,3,16,256]{3,2,1,0:T(8,128)S(1)}, f32[6,3,16,256]{3,2,1,0:T(8,128)S(1)}, u32[]{:S(2)}, u32[]{:S(2)}) collective-permute-start(f32[6,3,16,256]{3,2,1,0:T(8,128)S(1)} %get-tuple-element.71), channel_id=1, source_target_pairs={{0,0},{1,8},{2,16},{3,24},{4,32},{5,40},{6,48},{7,56},{8,64},{9,72... | collective-permute-start | bytes 884744 | tf_op jit(solution)/shard_map/ppermute | solution.py:328
  123.9 38.5 %collective-permute-start.5 = (f32[6,3,16,256]{3,2,1,0:T(8,128)S(1)}, f32[6,3,16,256]{3,2,1,0:T(8,128)S(1)}, u32[]{:S(2)}, u32[]{:S(2)}) collective-permute-start(f32[6,3,16,256]{3,2,1,0:T(8,128)S(1)} %get-tuple-element.71), channel_id=1, source_target_pairs={{0,64},{1,72},{2,80},{3,88},{4,96},{5,104},{6,112},{7,120},{8,0},{... | collective-permute-start | bytes 884744 | tf_op jit(solution)/shard_map/ppermute | solution.py:328
  127.2 35.3 %collective-permute-start.2 = (f32[6,3,16,256]{3,2,1,0:T(8,128)S(1)}, f32[6,3,16,256]{3,2,1,0:T(8,128)S(1)}, u32[]{:S(2)}, u32[]{:S(2)}) collective-permute-start(f32[6,3,16,256]{3,2,1,0:T(8,128)S(1)} %get-tuple-element.70), channel_id=1, source_target_pairs={{0,8},{1,0},{2,24},{3,16},{4,40},{5,32},{6,56},{7,48},{8,72},{9,64... | collective-permute-start | bytes 884744 | tf_op jit(solution)/shard_map/ppermute | solution.py:328
  133.5 29.0 %collective-permute-start.4 = (f32[6,3,16,256]{3,2,1,0:T(8,128)S(1)}, f32[6,3,16,256]{3,2,1,0:T(8,128)S(1)}, u32[]{:S(2)}, u32[]{:S(2)}) collective-permute-start(f32[6,3,16,256]{3,2,1,0:T(8,128)S(1)} %get-tuple-element.70), channel_id=1, source_target_pairs={{0,72},{1,64},{2,88},{3,80},{4,104},{5,96},{6,120},{7,112},{8,8},{... | collective-permute-start | bytes 884744 | tf_op jit(solution)/shard_map/ppermute | solution.py:328
  135.6 2.6 copy-start.19
  162.4 0.8 copy-start
  162.4 1.1 copy-start.1
  162.4 1.2 copy-start.2
  162.4 1.4 copy-start.3
  162.4 1.5 copy-start.4
  162.5 1.7 copy-start.9
  162.5 1.8 copy-start.10
  167.2 72.0 %all-to-all-start.3 = ((f32[4,2,6,3,32,256]{5,4,3,2,1,0:T(8,128)}), f32[4,2,6,3,32,256]{5,4,3,2,1,0:T(8,128)}, u32[]{:S(2)}, u32[]{:S(2)}) async-start(f32[4,2,6,3,32,256]{5,4,3,2,1,0:T(8,128)} %broadcast_in_dim.100), calls=%async_computation.3 | async-start | bytes 9437184 | tf_op jit(solution)/shard_map/all_to_all | solution.py:382
  173.7 52.6 %collective-permute-start.6 = (f32[4,256,256]{2,1,0:T(8,128)}, f32[4,256,256]{2,1,0:T(8,128)S(1)}, u32[]{:S(2)}, u32[]{:S(2)}) collective-permute-start(f32[4,256,256]{2,1,0:T(8,128)} %bitcast.206), channel_id=1, source_target_pairs={{6,70},{7,71},{8,72},{9,73},{10,74},{11,75},{12,76},{13,77},{14,78... | collective-permute-start | bytes 3145736 | tf_op jit(solution)/shard_map/ppermute | solution.py:328
  182.3 57.0 %collective-permute-start.7 = (f32[4,256,256]{2,1,0:T(8,128)}, f32[4,256,256]{2,1,0:T(8,128)}, u32[]{:S(2)}, u32[]{:S(2)}) collective-permute-start(f32[4,256,256]{2,1,0:T(8,128)} %get-tuple-element.64), channel_id=1, source_target_pairs={{0,64},{1,65},{2,66},{3,67},{4,68},{5,69},{6,70},{7,71},{8,72},{9,... | collective-permute-start | bytes 3145736 | tf_op jit(solution)/shard_map/ppermute | solution.py:328
  203.5 19.1 %copy-start.5 = (f32[2,256,256]{2,1,0:T(8,128)}, f32[2,256,256]{2,1,0:T(8,128)S(1)}, u32[]{:S(2)}) copy-start(f32[2,256,256]{2,1,0:T(8,128)S(1)} %get-tuple-element.59.refs_16_) | copy-start | bytes 1572868
  203.5 19.1 %copy-start.7 = (bf16[3,256,256]{2,1,0:T(8,128)(2,1)}, bf16[3,256,256]{2,1,0:T(8,128)(2,1)S(1)}, u32[]{:S(2)}) copy-start(bf16[3,256,256]{2,1,0:T(8,128)(2,1)S(1)} %get-tuple-element.47.refs_5_) | copy-start | bytes 1179652
  203.5 19.1 %copy-start.8 = (bf16[3,256,256]{2,1,0:T(8,128)(2,1)}, bf16[3,256,256]{2,1,0:T(8,128)(2,1)S(1)}, u32[]{:S(2)}) copy-start(bf16[3,256,256]{2,1,0:T(8,128)(2,1)S(1)} %get-tuple-element.48.refs_6_) | copy-start | bytes 1179652
  203.5 19.1 %copy-start.11 = (bf16[2,256,256]{2,1,0:T(8,128)(2,1)}, bf16[2,256,256]{2,1,0:T(8,128)(2,1)S(1)}, u32[]{:S(2)}) copy-start(bf16[2,256,256]{2,1,0:T(8,128)(2,1)S(1)} %get-tuple-element.49.refs_7_) | copy-start | bytes 786436
  203.6 19.1 %copy-start.12 = (bf16[2,256,256]{2,1,0:T(8,128)(2,1)}, bf16[2,256,256]{2,1,0:T(8,128)(2,1)S(1)}, u32[]{:S(2)}) copy-start(bf16[2,256,256]{2,1,0:T(8,128)(2,1)S(1)} %get-tuple-element.50.refs_8_) | copy-start | bytes 786436
  203.6 19.1 %copy-start.13 = (bf16[2,256,256]{2,1,0:T(8,128)(2,1)}, bf16[2,256,256]{2,1,0:T(8,128)(2,1)S(1)}, u32[]{:S(2)}) copy-start(bf16[2,256,256]{2,1,0:T(8,128)(2,1)S(1)} %get-tuple-element.57.refs_14_) | copy-start | bytes 786436
  203.6 19.1 %copy-start.14 = (bf16[2,256,256]{2,1,0:T(8,128)(2,1)}, bf16[2,256,256]{2,1,0:T(8,128)(2,1)S(1)}, u32[]{:S(2)}) copy-start(bf16[2,256,256]{2,1,0:T(8,128)(2,1)S(1)} %get-tuple-element.58.refs_15_) | copy-start | bytes 786436
  222.7 0.8 copy-start.6
  223.5 0.7 copy-start.15
  224.2 0.7 copy-start.16
  224.9 0.7 copy-start.17
  225.6 0.7 copy-start.18
  226.2 1.0 copy-start.23
Sparse Core Ops, SparseCore 0:
  56.0 47.1 all-gather.4
  118.6 87.4 all-gather.6

commit v3 on v2

--- a/solution.py
+++ b/solution.py
@@ -178,7 +178,7 @@
 ROW_TILE = 2
 
 
-CUTS = (0, 2, 4, 6)
+CUTS = (0, 6)
 LOWS = PANELS - 1
 PARTS = len(CUTS) - 1
 
@@ -206,8 +206,8 @@
     piece_ref, refs = refs[0], refs[1:]
     lows, refs = refs[:2 * LOWS], refs[2 * LOWS:]
     invs, refs = refs[:3 * PARTS], refs[3 * PARTS:]
-    shift_ref, child_ref, near_ref, rest_ref, late_ref, tail_ref, front_ref, out_ref = refs[:8]
-    x_ref, f_ref, rh_ref, rl_ref, ch_ref, cl_ref = refs[8:]
+    shift_ref, child_ref, lead_ref, late_ref, tail_ref, front_ref, out_ref = refs[:7]
+    x_ref, f_ref, rh_ref, rl_ref, ch_ref, cl_ref = refs[7:]
     r, c = place_ref[0], place_ref[1]
     side = r // HALF_ROWS
     step = pl.program_id(0)
@@ -275,7 +275,7 @@
                                 if u == 1:
                                     arrived = tail_ref[q]
                                 else:
-                                    arrived = late_ref[q] + (near_ref[0] if q == 0 else rest_ref[q - 1])
+                                    arrived = lead_ref[q] + late_ref[q]
                                 out_ref[here, there] += arrived
             level = p * N_ROW + r
 
@@ -290,7 +290,7 @@
                     out_ref[here, :BS] = invs[3 * i + 2][o]
 
 
-def finish(place, row_at, col_at, row_panel, col_panel, lows, invs, shift, child, near, rest, late, tail, front):
+def finish(place, row_at, col_at, row_panel, col_panel, lows, invs, shift, child, lead, late, tail, front):
     f32, bf = jnp.float32, jnp.bfloat16
     tiles = ROW_SLOTS // ROW_TILE
     whole = pl.BlockSpec(memory_space=pltpu.VMEM)
@@ -303,7 +303,7 @@
         grid=(tiles + 1,),
         in_specs=[smem] * 3
         + [pl.BlockSpec((N_COL, PANELS, ROW_TILE, STRIP, BS), lambda g: (0, 0, tile_at(g), 0, 0))]
-        + [whole] * (1 + 2 * LOWS + 3 * PARTS + 6)
+        + [whole] * (1 + 2 * LOWS + 3 * PARTS + 5)
         + [front_spec],
         out_specs=front_spec,
         out_shape=jax.ShapeDtypeStruct(front.shape, f32),
@@ -317,7 +317,7 @@
         ],
         compiler_params=pltpu.CompilerParams(vmem_limit_bytes=60 * 2**20),
         name="finish",
-    )(place, row_at, col_at, row_panel, col_panel, *lows, *invs, shift, child, near, rest, late, tail, front)
+    )(place, row_at, col_at, row_panel, col_panel, *lows, *invs, shift, child, lead, late, tail, front)
 
 
 def device(r, c):
@@ -347,7 +347,8 @@
         return jnp.where(first, child[:, 1, :, cols], child[:, 0, :, cols])
 
     lead = leaving(slice(0, BS))
-    near_in = swap_rows(lead[:1], HALF_ROWS, range(PANELS))
+    lead_in = swap_rows(lead, HALF_ROWS, range(PANELS))
+
     entry = jnp.arange(child_map.shape[1], dtype=jnp.int32)
     want_row = jnp.arange(CHILD_SLOTS, dtype=jnp.int32) * N_ROW + r
     want_col = jnp.arange(2, dtype=jnp.int32) * N_COL + c
@@ -370,8 +371,7 @@
         for h in range(2):
             for q in range(p % 2, CHILD_SLOTS, 2):
                 if 0 <= p - q <= 2:
-                    arrived = near_in[0] if q == 0 else rest_in[q - 1]
-                    part = jnp.where(first == (h == 0), staying[q], arrived)
+                    part = jnp.where(first == (h == 0), staying[q], lead_in[q])
                     hit = (col_at[h, 0] == 0) & (row_at[h, q] == p)
                     tile = tile + jnp.where(hit, part, 0.0)
         return tile.reshape(N_COL, STRIP, BS)
@@ -381,20 +381,13 @@
         groups = None if n == N_ROW else [list(g) for g in groups]
         return lax.all_to_all(jnp.broadcast_to(x, (n, *x.shape)), "row", 0, 0, axis_index_groups=groups)
 
-    strips = lax.all_to_all(raw_tile(0), "col", 0, 0)[:PANELS]
-    rest_in = swap_rows(after(lead[1:], strips), HALF_ROWS, range(PANELS))
-    near = row_gather(strips, range(N_ROW))
+    column = jnp.stack([raw_tile(p) for p in range(ROW_SLOTS)], axis=1)
+    dealt = lax.all_to_all(column, "col", 0, 0)[:PANELS]
+
+    near = row_gather(dealt[:, 0], range(N_ROW))
     packed = jnp.concatenate([near[i, : i + 1] for i in range(PANELS)], axis=0)
     top = lax.all_gather(packed, "col")
-
-    column = jnp.stack([raw_tile(p) for p in range(1, ROW_SLOTS)], axis=1)
-    dealt = lax.all_to_all(after(column, packed), "col", 0, 0)[:PANELS]
-    dealt = jnp.concatenate([strips[:, None], dealt], axis=1)
-
-    lows0, invs0, blocks0 = top_part(CUTS[0], CUTS[1], top)
-    lows1, invs1, blocks1 = top_part(CUTS[1], CUTS[2], blocks0)
-    lows2, invs2, _ = top_part(CUTS[2], CUTS[3], blocks1)
-    lows, invs = lows0 + lows1 + lows2, invs0 + invs1 + invs2
+    dealt = after(dealt, packed)
 
     even, odd = dealt[:, 0::2], dealt[:, 1::2]
     is_odd = c % 2 == 1
@@ -411,7 +404,7 @@
 
     pair = []
     for far in (0, 1):
-        straight, crossed = after(turned(0, far), blocks0), after(turned(1, far), blocks0)
+        straight, crossed = turned(0, far), turned(1, far)
         pair.append(
             jnp.concatenate([jnp.where(upper, crossed, straight), jnp.where(upper, straight, crossed)], axis=2)
         )
@@ -420,13 +413,20 @@
 
     row_panel = lax.all_gather(after(dealt, top), "col")
 
-    lead_late = swap_rows(after(lead, blocks0), HALF_ROWS, range(PANELS, N_COL))
-    tail_in = swap_rows(after(leaving(slice(BS, 2 * BS)), blocks0), HALF_ROWS, range(N_COL))
+    row_panel = lax.all_gather(dealt, "col")
+
+    lows, invs, blocks = [], [], after(top, pair)
+    for i in range(PARTS):
+        low, inv, blocks = top_part(CUTS[i], CUTS[i + 1], blocks)
+        lows, invs = lows + list(low), invs + list(inv)
+
+    lead_late = swap_rows(after(lead, pair), HALF_ROWS, range(PANELS, N_COL))
+    tail_in = swap_rows(after(leaving(slice(BS, 2 * BS)), pair), HALF_ROWS, range(N_COL))
 
     place = jnp.stack([r, c]).astype(jnp.int32)
     return finish(
         place, row_at.reshape(-1), col_at.reshape(-1), row_panel, col_panel, lows, invs,
-        pivot_shift.reshape(-1, BS), child, near_in, rest_in, lead_late, tail_in, front_orig,
+        pivot_shift.reshape(-1, BS), child, lead_in, lead_late, tail_in, front_orig,
     )
 
 

time: 297 us -> 297 us (level)
  blocking collectives: 85.1 us -> 58.9 us
  waiting for transfers between devices: 12.1 us -> 36.4 us
  local copies, waits for them, and re-layouts: 14.6 us -> 20.7 us
    all_to_all x2 -> x1, blocking collectives: 65 us -> 39 us  [on_device(): dealt = lax.all_to_all(column, 'col', 0, 0)[:PANELS]]
    all_gather x1, waiting for transfers between devices: 0.01 us -> 21.8 us  [on_device(): top = lax.all_gather(packed, 'col')]
    unnamed x63 -> x48, local copies, waits for them, and re-layouts: 9.49 us -> 14.9 us
    ppermute x8 -> x7, waiting for transfers between devices: 12 us -> 14.5 us  [permute(): return lax.ppermute(x, ('row', 'col'), pairs)]
    ppermute x8 -> x7, starting transfers between devices: 23.8 us -> 21.9 us  [permute(): return lax.ppermute(x, ('row', 'col'), pairs)]
    pallas_call x3 -> x1, Pallas kernels: 64.3 us -> 63.9 us  [top_part(): pl.pallas_call(lambda *refs: top_kernel(first, last, *refs), out_shape=sh...]
  transfers between devices with their start and end apart: 11 -> 10, of which waited for: 1 -> 4; matrix products, arithmetic and copies ran while one was open for 5% -> 4% of each run, Pallas kernels for 22% -> 22%
where the time goes in v3:
time: 297 us; the launch traced here: 294 us
  Pallas kernels  111 us (37%)
  blocking collectives  58.9 us (20%)
  waiting for transfers between devices  36.4 us (12%)
  starting transfers between devices  29.5 us (10%)
  between operations  25.1 us (8%)
  local copies, waits for them, and re-layouts  20.7 us (7%)
  other arithmetic  12.8 us (4%)
    pallas_call x1, Pallas kernels, top_part(): pl.pallas_call(lambda *refs: top_kernel(first, last, *refs), out_shape=sh...  63.9 us
    pallas_call x1, Pallas kernels, finish(): pl.pallas_call(rows_kernel, grid=(tiles + 1,), in_specs=[smem] * 3 + [pl....  47.1 us
    all_to_all x1, blocking collectives, on_device(): dealt = lax.all_to_all(column, 'col', 0, 0)[:PANELS]  39 us
    ppermute x7, starting transfers between devices, permute(): return lax.ppermute(x, ('row', 'col'), pairs)  21.9 us
    all_gather x1, waiting for transfers between devices, on_device(): top = lax.all_gather(packed, 'col')  21.8 us
    all_to_all x1, blocking collectives, row_gather(): lax.all_to_all(jnp.broadcast_to(x, (n, *x.shape)), 'row', 0, 0, axis_inde...  19.9 us
    unnamed x48, local copies, waits for them, and re-layouts  14.9 us
    ppermute x7, waiting for transfers between devices, permute(): return lax.ppermute(x, ('row', 'col'), pairs)  14.5 us
  transfers between devices with their start and end apart: 10, of which 4 were waited for; matrix products, arithmetic and copies ran while one was open for 4% of the time, Pallas kernels for 22%

profile of v3, /device:TPU:10, one launch (start us, length us, event | category | flops | bytes accessed | tf_op | source)
XLA Modules:
  0.0 294.3 jit_solution(5152250718117612881)
XLA Ops:
  6.5 3.6 %fusion.1 = (f32[4,256,256]{2,1,0:T(8,128)S(1)}, f32[4,256,256]{2,1,0:T(8,128)}) fusion(f32[4,2,256,512]{3,2,1,0:T(8,128)} %bitcast.201, pred[]{:T(512)S(6)} %lt.14), kind=kLoop, calls=%fused_computation.3 | loop fusion | flops 524288 | bytes 6291457 | tf_op jit(solution)/shard_map/jit(_where)/select_n | solution.py:347
  10.1 0.7 collective-permute-start
  10.9 0.1 iota_compare_fusion.1
  10.9 0.1 select_reduce_fusion
  11.1 0.7 fusion.17
  21.7 0.1 iota_compare_fusion.2
  21.7 0.1 select_reduce_fusion.1
  21.9 0.6 fusion.18
  24.0 1.7 bitcast_select_fusion.1
  25.7 0.0 collective-permute-done.refs_16_
  25.7 1.6 bitcast_add_fusion.4
  27.3 1.3 bitcast_add_fusion
  28.7 1.1 bitcast_add_fusion.8
  29.8 39.0 %all_to_all.15 = f32[16,6,16,256]{3,2,1,0:T(8,128)S(1)} all-to-all(f32[16,6,16,256]{3,2,1,0:T(8,128)S(1)} %constant_dynamic-update-slice_fusion), channel_id=1, replica_groups=mesh['row'=8,'col'=16] {'col'}, dimensions={0} | all-to-all | bytes 3145728 | tf_op jit(solution)/shard_map/all_to_all | solution.py:385
  68.9 0.1 broadcast_in_dim.95
  69.0 19.9 %all_to_all.16 = f32[8,6,16,256]{3,2,1,0:T(8,128)S(1)} all-to-all(f32[8,6,16,256]{3,2,1,0:T(8,128)S(1)} %broadcast_in_dim.95), channel_id=1, replica_groups=mesh['row'=8,'col'=16] {'row'}, dimensions={0} | all-to-all | bytes 1572864 | tf_op jit(solution)/shard_map/all_to_all | solution.py:382
  89.0 0.7 copy-done.16
  89.7 0.0 all-gather.7.cloned.1.call-update
  89.7 0.0 all-gather.5.cloned.1.call-start
  89.8 0.9 slice.232
  90.6 0.0 all-gather.5.cloned.1.call-update
  90.7 0.1 reduce_sum.23
  90.7 0.1 reduce_sum.25
  90.8 0.6 and_select_fusion.3.row_at_ref
  91.4 1.1 slice_select_fusion.1
  92.5 1.9 collective-permute-start.3
  94.5 1.9 collective-permute-start.4
  96.4 0.6 and_select_fusion.2.col_at_ref
  97.0 6.8 %collective-permute-start.1 = (f32[6,3,16,256]{3,2,1,0:T(8,128)S(1)}, f32[6,3,16,256]{3,2,1,0:T(8,128)S(1)}, u32[]{:S(2)}, u32[]{:S(2)}) collective-permute-start(f32[6,3,16,256]{3,2,1,0:T(8,128)S(1)} %get-tuple-element.50), channel_id=1, source_target_pairs={{0,8},{1,0},{2,24},{3,16},{4,40},{5,32},{6,56},{7,48},{8,72},{9,64... | collective-permute-start | bytes 884744 | tf_op jit(solution)/shard_map/ppermute | solution.py:328
  103.8 4.8 %collective-permute-start.2 = (f32[6,3,16,256]{3,2,1,0:T(8,128)S(1)}, f32[6,3,16,256]{3,2,1,0:T(8,128)S(1)}, u32[]{:S(2)}, u32[]{:S(2)}) collective-permute-start(f32[6,3,16,256]{3,2,1,0:T(8,128)S(1)} %get-tuple-element.51), channel_id=1, source_target_pairs={{0,0},{1,8},{2,16},{3,24},{4,32},{5,40},{6,48},{7,56},{8,64},{9,72... | collective-permute-start | bytes 884744 | tf_op jit(solution)/shard_map/ppermute | solution.py:328
  108.6 0.6 pad_add_fusion.place_ref
  109.2 0.6 reshape.201.refs_14_
  109.8 0.0 collective-permute-done.3
  109.8 2.1 collective-permute-done.4
  111.9 6.5 %collective-permute-done.1 = f32[6,3,16,256]{3,2,1,0:T(8,128)S(1)} collective-permute-done((f32[6,3,16,256]{3,2,1,0:T(8,128)S(1)}, f32[6,3,16,256]{3,2,1,0:T(8,128)S(1)}, u32[]{:S(2)}, u32[]{:S(2)}) %collective-permute-start.1) | collective-permute-done | bytes 294944 | tf_op jit(solution)/shard_map/ppermute | solution.py:328
  118.5 6.0 %collective-permute-done.2 = f32[6,3,16,256]{3,2,1,0:T(8,128)S(1)} collective-permute-done((f32[6,3,16,256]{3,2,1,0:T(8,128)S(1)}, f32[6,3,16,256]{3,2,1,0:T(8,128)S(1)}, u32[]{:S(2)}, u32[]{:S(2)}) %collective-permute-start.2) | collective-permute-done | bytes 294944 | tf_op jit(solution)/shard_map/ppermute | solution.py:328
  124.5 0.1 maximum_bitcast_fusion
  124.6 0.1 pad_maximum_fusion
  124.7 2.8 broadcast_in_dim.96
  127.4 7.5 %all-to-all-start.2 = ((f32[4,2,6,3,32,256]{5,4,3,2,1,0:T(8,128)}), f32[4,2,6,3,32,256]{5,4,3,2,1,0:T(8,128)}, u32[]{:S(2)}, u32[]{:S(2)}) async-start(f32[4,2,6,3,32,256]{5,4,3,2,1,0:T(8,128)} %broadcast_in_dim.96), calls=%async_computation.2 | async-start | bytes 9437184 | tf_op jit(solution)/shard_map/all_to_all | solution.py:382
  135.0 3.5 %collective-permute-start.5 = (f32[4,256,256]{2,1,0:T(8,128)}, f32[4,256,256]{2,1,0:T(8,128)S(1)}, u32[]{:S(2)}, u32[]{:S(2)}) collective-permute-start(f32[4,256,256]{2,1,0:T(8,128)} %get-tuple-element.37), channel_id=1, source_target_pairs={{6,70},{7,71},{8,72},{9,73},{10,74},{11,75},{12,76},{13,77},{14,78... | collective-permute-start | bytes 3145736 | tf_op jit(solution)/shard_map/ppermute | solution.py:328
  138.4 2.2 collective-permute-start.6
  140.7 21.8 %all-gather.7.cloned.1.call-done = f32[336,16,256]{2,1,0:T(8,128)} async-done(((f32[21,16,256]{2,1,0:T(8,128)}), f32[336,16,256]{2,1,0:T(8,128)}) %all-gather.7.cloned.1.call-update) | async-done | bytes 5505040 | tf_op jit(solution)/shard_map/all_gather | solution.py:389
  162.5 2.6 copy-done.13
  165.0 63.9 %top0.1 = (bf16[5,256,256]{2,1,0:T(8,128)(2,1)S(1)}, bf16[5,256,256]{2,1,0:T(8,128)(2,1)S(1)}, bf16[4,256,256]{2,1,0:T(8,128)(2,1)S(1)}, bf16[4,256,256]{2,1,0:T...) custom-call(f32[16,21,16,256]{3,2,1,0:T(8,128)S(1)} %bitcast.200), custom_call_target="tpu_custom_call" | custom-call | flops 65999998976 | bytes 240000000 | tf_op jit(solution)/shard_map/top0/pallas_call | solution.py:156
  228.9 1.1 copy-done
  230.1 0.9 copy-done.1
  230.9 0.9 copy-done.2
  231.9 0.9 copy-done.3
  232.7 0.8 copy-done.4
  233.6 0.8 copy-done.5
  234.4 0.8 copy-done.6
  235.2 0.7 copy-done.7
  235.9 0.8 copy-done.8
  236.7 0.7 copy-done.9
  237.4 0.7 copy-done.10
  238.1 0.6 copy-done.11
  238.8 0.6 copy-done.12
  239.4 0.0 collective-permute-done.5.refs_17_
  239.4 0.0 collective-permute-done.6.refs_18_
  239.4 0.0 all-to-all-done.2.refs_0_
  239.4 0.0 all-gather.5.cloned.1.call-done
  239.5 0.9 copy-done.15
  240.4 47.1 %finish.1 = f32[1536,768]{1,0:T(8,128)} custom-call(s32[2]{0:T(128)} %pad_add_fusion.place_ref, s32[8]{0:T(128)} %and_select_fusion.3.row_at_ref, s32[4]{0:T(128)} %and_select_fusion.2.col_at_ref, f32[16,6,6,16,256]{4,3,2,1,0:T(8,128)} %bitcast.204, f32[4,2,6,3,32,256]{5,4,3,2,1,0:T(8,128)} %all-to-all-done.2.refs_0_, bf16[5,256,256]{2,1,0:T(8,128)(2,1)} %copy-done.3, ...), custom_call_target="tpu_custom_call" | custom-call | tf_op jit(solution)/shard_map/finish/pallas_call | solution.py:301
  (44 shorter events, 0.4 us)
Async XLA Ops:
  6.5 155.9 %all-gather.7.cloned.1.call-start = ((), (), s32[]{:S(2)}) async-start(), calls=%async_computation.4 | async-start | bytes 5849088 | tf_op jit(solution)/shard_map/all_gather | solution.py:389
  6.5 4.4 %copy-start.18 = (s32[2,32]{1,0:T(2,128)S(1)}, s32[2,32]{1,0:T(2,128)}, u32[]{:S(2)}) copy-start(s32[2,32]{1,0:T(2,128)} %param.7) | copy-start | bytes 772
  6.5 17.3 %copy-start.17 = (f32[12288]{0:T(1024)S(1)}, f32[12288]{0:T(1024)}, u32[]{:S(2)}) copy-start(f32[12288]{0:T(1024)} %param.5) | copy-start | bytes 147460
  10.1 15.6 %collective-permute-start = (f32[4,256,256]{2,1,0:T(8,128)}, f32[4,256,256]{2,1,0:T(8,128)S(1)}, u32[]{:S(2)}, u32[]{:S(2)}) collective-permute-start(f32[4,256,256]{2,1,0:T(8,128)} %get-tuple-element.37), channel_id=1, source_target_pairs={{0,64},{1,65},{2,66},{3,67},{4,68},{5,69},{16,80},{17,81},{18,82},... | collective-permute-start | bytes 3145736 | tf_op jit(solution)/shard_map/ppermute | solution.py:328
  25.7 3.0 %copy-start.14 = (f32[4,256,256]{2,1,0:T(8,128)}, f32[4,256,256]{2,1,0:T(8,128)S(1)}, u32[]{:S(2)}) copy-start(f32[4,256,256]{2,1,0:T(8,128)S(1)} %collective-permute-done.refs_16_) | copy-start | bytes 3145732
  88.9 0.7 copy-start.16
  89.7 149.8 %all-gather.5.cloned.1.call-start = ((), (), s32[]{:S(2)}) async-start(), calls=%async_computation.3 | async-start | bytes 10027008 | tf_op jit(solution)/shard_map/all_gather | solution.py:416
  92.5 17.3 %collective-permute-start.3 = (f32[6,3,16,256]{3,2,1,0:T(8,128)S(1)}, f32[6,3,16,256]{3,2,1,0:T(8,128)S(1)}, u32[]{:S(2)}, u32[]{:S(2)}) collective-permute-start(f32[6,3,16,256]{3,2,1,0:T(8,128)S(1)} %get-tuple-element.50), channel_id=1, source_target_pairs={{0,72},{1,64},{2,88},{3,80},{4,104},{5,96},{6,120},{7,112},{8,8},{... | collective-permute-start | bytes 884744 | tf_op jit(solution)/shard_map/ppermute | solution.py:328
  94.5 17.4 %collective-permute-start.4 = (f32[6,3,16,256]{3,2,1,0:T(8,128)S(1)}, f32[6,3,16,256]{3,2,1,0:T(8,128)S(1)}, u32[]{:S(2)}, u32[]{:S(2)}) collective-permute-start(f32[6,3,16,256]{3,2,1,0:T(8,128)S(1)} %get-tuple-element.51), channel_id=1, source_target_pairs={{0,64},{1,72},{2,80},{3,88},{4,96},{5,104},{6,112},{7,120},{8,0},{... | collective-permute-start | bytes 884744 | tf_op jit(solution)/shard_map/ppermute | solution.py:328
  97.0 21.5 %collective-permute-start.1 = (f32[6,3,16,256]{3,2,1,0:T(8,128)S(1)}, f32[6,3,16,256]{3,2,1,0:T(8,128)S(1)}, u32[]{:S(2)}, u32[]{:S(2)}) collective-permute-start(f32[6,3,16,256]{3,2,1,0:T(8,128)S(1)} %get-tuple-element.50), channel_id=1, source_target_pairs={{0,8},{1,0},{2,24},{3,16},{4,40},{5,32},{6,56},{7,48},{8,72},{9,64... | collective-permute-start | bytes 884744 | tf_op jit(solution)/shard_map/ppermute | solution.py:328
  103.8 20.6 %collective-permute-start.2 = (f32[6,3,16,256]{3,2,1,0:T(8,128)S(1)}, f32[6,3,16,256]{3,2,1,0:T(8,128)S(1)}, u32[]{:S(2)}, u32[]{:S(2)}) collective-permute-start(f32[6,3,16,256]{3,2,1,0:T(8,128)S(1)} %get-tuple-element.51), channel_id=1, source_target_pairs={{0,0},{1,8},{2,16},{3,24},{4,32},{5,40},{6,48},{7,56},{8,64},{9,72... | collective-permute-start | bytes 884744 | tf_op jit(solution)/shard_map/ppermute | solution.py:328
  127.4 112.0 %all-to-all-start.2 = ((f32[4,2,6,3,32,256]{5,4,3,2,1,0:T(8,128)}), f32[4,2,6,3,32,256]{5,4,3,2,1,0:T(8,128)}, u32[]{:S(2)}, u32[]{:S(2)}) async-start(f32[4,2,6,3,32,256]{5,4,3,2,1,0:T(8,128)} %broadcast_in_dim.96), calls=%async_computation.2 | async-start | bytes 9437184 | tf_op jit(solution)/shard_map/all_to_all | solution.py:382
  135.0 104.5 %collective-permute-start.5 = (f32[4,256,256]{2,1,0:T(8,128)}, f32[4,256,256]{2,1,0:T(8,128)S(1)}, u32[]{:S(2)}, u32[]{:S(2)}) collective-permute-start(f32[4,256,256]{2,1,0:T(8,128)} %get-tuple-element.37), channel_id=1, source_target_pairs={{6,70},{7,71},{8,72},{9,73},{10,74},{11,75},{12,76},{13,77},{14,78... | collective-permute-start | bytes 3145736 | tf_op jit(solution)/shard_map/ppermute | solution.py:328
  138.4 101.0 %collective-permute-start.6 = (f32[4,256,256]{2,1,0:T(8,128)S(1)}, f32[4,256,256]{2,1,0:T(8,128)}, u32[]{:S(2)}, u32[]{:S(2)}) collective-permute-start(f32[4,256,256]{2,1,0:T(8,128)S(1)} %get-tuple-element.38), channel_id=1, source_target_pairs={{0,64},{1,65},{2,66},{3,67},{4,68},{5,69},{6,70},{7,71},{8,72},{9,... | collective-permute-start | bytes 3145736 | tf_op jit(solution)/shard_map/ppermute | solution.py:328
  162.5 2.6 copy-start.13
  228.9 1.1 copy-start
  230.0 0.9 copy-start.1
  230.9 0.9 copy-start.2
  231.8 0.9 copy-start.3
  232.7 0.8 copy-start.4
  233.6 0.8 copy-start.5
  234.4 0.8 copy-start.6
  235.2 0.7 copy-start.7
  235.9 0.8 copy-start.8
  236.7 0.7 copy-start.9
  237.4 0.7 copy-start.10
  238.1 0.6 copy-start.11
  238.8 0.6 copy-start.12
  239.4 1.0 copy-start.15
Sparse Core Ops, SparseCore 0:
  89.8 72.5 all-gather.6
  164.2 72.8 all-gather.4

commit v4 on v3

--- a/solution.py
+++ b/solution.py
@@ -75,8 +75,12 @@
 LEAF = 128
 
 
+def low_at(k, i):
+    return sum(PANELS - 1 - m for m in range(k)) + i - k - 1
+
+
 def top_kernel(first, last, in_ref, *refs):
-    lows, refs = refs[:2 * (min(last, PANELS - 1) - first)], refs[2 * (min(last, PANELS - 1) - first):]
+    lh_ref, ll_ref, refs = refs[0], refs[1], refs[2:]
     ih_ref, il_ref, fac_ref, refs = refs[0], refs[1], refs[2], refs[3:]
     if last < PANELS:
         on_ref, refs = refs[0], refs[1:]
@@ -126,8 +130,8 @@
                 rest = PANELS - 1 - at
                 below = a_ref[at * PANELS + at + 1:(at + 1) * PANELS].reshape(rest * BS, BS)
                 xh, xl = split(dot3(*split(below), ih, il))
-                lows[2 * (at - first)][...] = xh.reshape(rest, BS, BS)
-                lows[2 * (at - first) + 1][...] = xl.reshape(rest, BS, BS)
+                lh_ref[low_at(at, at + 1):low_at(at, PANELS)] = xh.reshape(rest, BS, BS)
+                ll_ref[low_at(at, at + 1):low_at(at, PANELS)] = xl.reshape(rest, BS, BS)
                 for j in range(at + 1, PANELS):
                     o = (j - at - 1) * BS
                     old = a_ref[j * PANELS + j:(j + 1) * PANELS]
@@ -145,9 +149,7 @@
 def top_part(first, last, blocks):
     f32, bf = jnp.float32, jnp.bfloat16
     n = last - first
-    shapes = []
-    for at in range(first, min(last, PANELS - 1)):
-        shapes += [jax.ShapeDtypeStruct((PANELS - 1 - at, BS, BS), bf)] * 2
+    shapes = [jax.ShapeDtypeStruct((PANELS * (PANELS - 1) // 2, BS, BS), bf)] * 2
     low_count = len(shapes)
     shapes += [jax.ShapeDtypeStruct((n, BS, BS), bf)] * 2 + [jax.ShapeDtypeStruct((n, BS, BS), f32)]
     left = PANELS - last
@@ -179,7 +181,6 @@
 
 
 CUTS = (0, 6)
-LOWS = PANELS - 1
 PARTS = len(CUTS) - 1
 
 
@@ -192,7 +193,7 @@
     for k in range(PANELS):
         acc = x_ref[k, :rows]
         for m in range(k):
-            acc = acc - dot3(h_ref[m], l_ref[m], lows[2 * m][k - m - 1], lows[2 * m + 1][k - m - 1])
+            acc = acc - dot3(h_ref[m], l_ref[m], lows[0][low_at(m, k)], lows[1][low_at(m, k)])
         i, o = part_of(k)
         out = dot3(*split(acc), invs[3 * i][o], invs[3 * i + 1][o])
         hi, lo = split(out)
@@ -204,10 +205,10 @@
 
 def rows_kernel(place_ref, row_at_ref, col_at_ref, row_ref, *refs):
     piece_ref, refs = refs[0], refs[1:]
-    lows, refs = refs[:2 * LOWS], refs[2 * LOWS:]
+    lows, refs = refs[:2], refs[2:]
     invs, refs = refs[:3 * PARTS], refs[3 * PARTS:]
-    shift_ref, child_ref, lead_ref, late_ref, tail_ref, front_ref, out_ref = refs[:7]
-    x_ref, f_ref, rh_ref, rl_ref, ch_ref, cl_ref = refs[7:]
+    shift_ref, child_ref, other_ref, front_ref, out_ref = refs[:5]
+    x_ref, f_ref, rh_ref, rl_ref, ch_ref, cl_ref = refs[5:]
     r, c = place_ref[0], place_ref[1]
     side = r // HALF_ROWS
     step = pl.program_id(0)
@@ -272,10 +273,7 @@
 
                             @pl.when(hit & (side != h))
                             def _(here=here, there=there, q=q, u=u):
-                                if u == 1:
-                                    arrived = tail_ref[q]
-                                else:
-                                    arrived = lead_ref[q] + late_ref[q]
+                                arrived = other_ref[q, :, u * BS:(u + 1) * BS]
                                 out_ref[here, there] += arrived
             level = p * N_ROW + r
 
@@ -290,7 +288,7 @@
                     out_ref[here, :BS] = invs[3 * i + 2][o]
 
 
-def finish(place, row_at, col_at, row_panel, col_panel, lows, invs, shift, child, lead, late, tail, front):
+def finish(place, row_at, col_at, row_panel, col_panel, lows, invs, shift, child, other, front):
     f32, bf = jnp.float32, jnp.bfloat16
     tiles = ROW_SLOTS // ROW_TILE
     whole = pl.BlockSpec(memory_space=pltpu.VMEM)
@@ -303,7 +301,7 @@
         grid=(tiles + 1,),
         in_specs=[smem] * 3
         + [pl.BlockSpec((N_COL, PANELS, ROW_TILE, STRIP, BS), lambda g: (0, 0, tile_at(g), 0, 0))]
-        + [whole] * (1 + 2 * LOWS + 3 * PARTS + 5)
+        + [whole] * (1 + 2 + 3 * PARTS + 3)
         + [front_spec],
         out_specs=front_spec,
         out_shape=jax.ShapeDtypeStruct(front.shape, f32),
@@ -317,7 +315,7 @@
         ],
         compiler_params=pltpu.CompilerParams(vmem_limit_bytes=60 * 2**20),
         name="finish",
-    )(place, row_at, col_at, row_panel, col_panel, *lows, *invs, shift, child, lead, late, tail, front)
+    )(place, row_at, col_at, row_panel, col_panel, *lows, *invs, shift, child, other, front)
 
 
 def device(r, c):
@@ -384,6 +382,8 @@
     column = jnp.stack([raw_tile(p) for p in range(ROW_SLOTS)], axis=1)
     dealt = lax.all_to_all(column, "col", 0, 0)[:PANELS]
 
+    other = swap_rows(after(leaving(slice(0, 2 * BS)), dealt), HALF_ROWS, range(N_COL))
+
     near = row_gather(dealt[:, 0], range(N_ROW))
     packed = jnp.concatenate([near[i, : i + 1] for i in range(PANELS)], axis=0)
     top = lax.all_gather(packed, "col")
@@ -420,13 +420,10 @@
         low, inv, blocks = top_part(CUTS[i], CUTS[i + 1], blocks)
         lows, invs = lows + list(low), invs + list(inv)
 
-    lead_late = swap_rows(after(lead, pair), HALF_ROWS, range(PANELS, N_COL))
-    tail_in = swap_rows(after(leaving(slice(BS, 2 * BS)), pair), HALF_ROWS, range(N_COL))
-
     place = jnp.stack([r, c]).astype(jnp.int32)
     return finish(
         place, row_at.reshape(-1), col_at.reshape(-1), row_panel, col_panel, lows, invs,
-        pivot_shift.reshape(-1, BS), child, lead_in, lead_late, tail_in, front_orig,
+        pivot_shift.reshape(-1, BS), child, other, front_orig,
     )
 
 

time: 297 us -> 294 us (0.990)
  local copies, waits for them, and re-layouts: 20.7 us -> 14.9 us
  waiting for transfers between devices: 36.4 us -> 41 us
    all_gather x1, waiting for transfers between devices: 21.8 us -> 29.2 us  [on_device(): top = lax.all_gather(packed, 'col')]
    unnamed x48 -> x30, local copies, waits for them, and re-layouts: 14.9 us -> 9.06 us
    ppermute x7 -> x6, starting transfers between devices: 21.9 us -> 18.1 us  [permute(): return lax.ppermute(x, ('row', 'col'), pairs)]
    ppermute x7 -> x6, waiting for transfers between devices: 14.5 us -> 11.7 us  [permute(): return lax.ppermute(x, ('row', 'col'), pairs)]
  transfers between devices with their start and end apart: 10 -> 9, of which waited for: 4 -> 4; matrix products, arithmetic and copies ran while one was open for 4% -> 4% of each run, Pallas kernels for 22% -> 22%
where the time goes in v4:
time: 294 us; the launch traced here: 291 us
  Pallas kernels  111 us (38%)
  blocking collectives  60.1 us (20%)
  waiting for transfers between devices  41 us (14%)
  starting transfers between devices  26.6 us (9%)
  between operations  25.3 us (9%)
  local copies, waits for them, and re-layouts  14.9 us (5%)
  other arithmetic  12.6 us (4%)
    pallas_call x1, Pallas kernels, top_part(): pl.pallas_call(lambda *refs: top_kernel(first, last, *refs), out_shape=sh...  63.9 us
    pallas_call x1, Pallas kernels, finish(): pl.pallas_call(rows_kernel, grid=(tiles + 1,), in_specs=[smem] * 3 + [pl....  46.7 us
    all_to_all x1, blocking collectives, on_device(): dealt = lax.all_to_all(column, 'col', 0, 0)[:PANELS]  40.2 us
    all_gather x1, waiting for transfers between devices, on_device(): top = lax.all_gather(packed, 'col')  29.2 us
    all_to_all x1, blocking collectives, row_gather(): lax.all_to_all(jnp.broadcast_to(x, (n, *x.shape)), 'row', 0, 0, axis_inde...  19.9 us
    ppermute x6, starting transfers between devices, permute(): return lax.ppermute(x, ('row', 'col'), pairs)  18.1 us
    ppermute x6, waiting for transfers between devices, permute(): return lax.ppermute(x, ('row', 'col'), pairs)  11.7 us
    unnamed x30, local copies, waits for them, and re-layouts  9.06 us
  transfers between devices with their start and end apart: 9, of which 4 were waited for; matrix products, arithmetic and copies ran while one was open for 4% of the time, Pallas kernels for 22%

profile of v4, /device:TPU:10, one launch (start us, length us, event | category | flops | bytes accessed | tf_op | source)
XLA Modules:
  0.0 291.2 jit_solution(6017917029726193069)
XLA Ops:
  6.5 0.0 all-gather.7.cloned.1.call-start
  6.5 0.0 copy-start.9
  6.5 0.0 copy-start.8
  6.5 1.8 slice_select_fusion
  8.3 0.7 collective-permute-start
  9.1 0.1 iota_compare_fusion.1
  9.1 0.0 copy-done.9
  9.2 0.1 select_reduce_fusion
  9.3 0.7 fusion.16
  20.2 0.1 iota_compare_fusion.2
  20.3 0.1 select_reduce_fusion.1
  20.4 0.6 fusion.17
  22.4 0.0 copy-done.8
  22.5 0.0 collective-permute-done
  22.5 1.2 bitcast_add_fusion.4
  23.8 1.3 bitcast_add_fusion
  25.1 1.1 bitcast_add_fusion.8
  26.3 40.2 %all_to_all.15 = f32[16,6,16,256]{3,2,1,0:T(8,128)S(1)} all-to-all(f32[16,6,16,256]{3,2,1,0:T(8,128)S(1)} %constant_dynamic-update-slice_fusion), channel_id=1, replica_groups=mesh['row'=8,'col'=16] {'col'}, dimensions={0} | all-to-all | bytes 3145728 | tf_op jit(solution)/shard_map/all_to_all | solution.py:383
  66.5 0.1 broadcast_in_dim.95
  66.6 19.9 %all_to_all.16 = f32[8,6,16,256]{3,2,1,0:T(8,128)S(1)} all-to-all(f32[8,6,16,256]{3,2,1,0:T(8,128)S(1)} %broadcast_in_dim.95), channel_id=1, replica_groups=mesh['row'=8,'col'=16] {'row'}, dimensions={0} | all-to-all | bytes 1572864 | tf_op jit(solution)/shard_map/all_to_all | solution.py:380
  86.6 0.0 copy-start.7
  86.6 0.7 copy-done.7
  87.3 0.0 all-gather.7.cloned.1.call-update
  87.4 0.0 all-gather.5.cloned.1.call-start
  87.4 0.9 slice.232
  88.3 0.0 all-gather.5.cloned.1.call-update
  88.3 0.1 reduce_sum.23
  88.4 0.1 reduce_sum.25
  88.5 0.5 and_select_fusion.3.row_at_ref
  89.0 2.8 fusion.1
  91.8 0.0 copy-done.6
  91.8 0.1 slice_select_fusion.2
  91.8 1.9 collective-permute-start.3
  93.8 1.9 collective-permute-start.4
  95.7 0.6 and_select_fusion.2.col_at_ref
  96.3 6.8 %collective-permute-start.1 = (f32[6,3,16,256]{3,2,1,0:T(8,128)S(1)}, f32[6,3,16,256]{3,2,1,0:T(8,128)S(1)}, u32[]{:S(2)}, u32[]{:S(2)}) collective-permute-start(f32[6,3,16,256]{3,2,1,0:T(8,128)S(1)} %get-tuple-element.32), channel_id=1, source_target_pairs={{0,8},{1,0},{2,24},{3,16},{4,40},{5,32},{6,56},{7,48},{8,72},{9,64... | collective-permute-start | bytes 884744 | tf_op jit(solution)/shard_map/ppermute | solution.py:326
  103.1 4.8 %collective-permute-start.2 = (f32[6,3,16,256]{3,2,1,0:T(8,128)S(1)}, f32[6,3,16,256]{3,2,1,0:T(8,128)}, u32[]{:S(2)}, u32[]{:S(2)}) collective-permute-start(f32[6,3,16,256]{3,2,1,0:T(8,128)S(1)} %get-tuple-element.33), channel_id=1, source_target_pairs={{0,0},{1,8},{2,16},{3,24},{4,32},{5,40},{6,48},{7,56},{8,64},{9,72... | collective-permute-start | bytes 884744 | tf_op jit(solution)/shard_map/ppermute | solution.py:326
  107.9 0.7 pad_add_fusion.place_ref
  108.6 0.6 reshape.201.refs_6_
  109.2 1.9 collective-permute-start.5
  111.1 0.0 collective-permute-done.3
  111.1 0.2 collective-permute-done.4
  111.3 1.0 broadcast_select_fusion.1
  112.3 5.6 %collective-permute-done.1 = f32[6,3,16,256]{3,2,1,0:T(8,128)S(1)} collective-permute-done((f32[6,3,16,256]{3,2,1,0:T(8,128)S(1)}, f32[6,3,16,256]{3,2,1,0:T(8,128)S(1)}, u32[]{:S(2)}, u32[]{:S(2)}) %collective-permute-start.1) | collective-permute-done | bytes 294944 | tf_op jit(solution)/shard_map/ppermute | solution.py:326
  117.9 6.0 %collective-permute-done.2 = f32[6,3,16,256]{3,2,1,0:T(8,128)} collective-permute-done((f32[6,3,16,256]{3,2,1,0:T(8,128)S(1)}, f32[6,3,16,256]{3,2,1,0:T(8,128)}, u32[]{:S(2)}, u32[]{:S(2)}) %collective-permute-start.2) | collective-permute-done | bytes 294944 | tf_op jit(solution)/shard_map/ppermute | solution.py:326
  123.8 1.0 broadcast_select_fusion.3
  124.8 0.1 maximum_bitcast_fusion
  124.9 0.1 pad_maximum_fusion
  125.0 2.8 broadcast_in_dim.96
  127.8 8.5 %all-to-all-start.2 = ((f32[4,2,6,3,32,256]{5,4,3,2,1,0:T(8,128)}), f32[4,2,6,3,32,256]{5,4,3,2,1,0:T(8,128)}, u32[]{:S(2)}, u32[]{:S(2)}) async-start(f32[4,2,6,3,32,256]{5,4,3,2,1,0:T(8,128)} %broadcast_in_dim.96), calls=%async_computation.2 | async-start | bytes 9437184 | tf_op jit(solution)/shard_map/all_to_all | solution.py:380
  136.3 29.2 %all-gather.7.cloned.1.call-done = f32[336,16,256]{2,1,0:T(8,128)} async-done(((f32[21,16,256]{2,1,0:T(8,128)}), f32[336,16,256]{2,1,0:T(8,128)}) %all-gather.7.cloned.1.call-update) | async-done | bytes 5505040 | tf_op jit(solution)/shard_map/all_gather | solution.py:389
  165.5 0.0 copy-start.5
  165.5 2.6 copy-done.5
  168.1 63.9 %top0.1 = (bf16[15,256,256]{2,1,0:T(8,128)(2,1)S(1)}, bf16[15,256,256]{2,1,0:T(8,128)(2,1)S(1)}, bf16[6,256,256]{2,1,0:T(8,128)(2,1)S(1)}, bf16[6,256,256]{2,1,0:T(8,128)(2,1)S(1)}, f32[6,256,256]{2,1,0:T(8,128)S(1)}) custom-call(f32[16,21,16,256]{3,2,1,0:T(8,128)S(1)} %bitcast.192), custom_call_target="tpu_custom_call" | custom-call | flops 65999998976 | bytes 240000000 | tf_op jit(solution)/shard_map/top0/pallas_call | solution.py:158
  232.0 0.0 copy-start
  232.0 1.3 copy-done
  233.3 1.4 copy-done.1
  234.7 0.0 copy-start.2
  234.7 1.1 copy-done.2
  235.8 0.9 copy-done.3
  236.7 0.9 copy-done.4
  237.6 0.0 collective-permute-done.5.refs_8_
  237.6 0.0 all-to-all-done.2.refs_0_
  237.6 46.7 %finish.1 = f32[1536,768]{1,0:T(8,128)} custom-call(s32[2]{0:T(128)} %pad_add_fusion.place_ref, s32[8]{0:T(128)} %and_select_fusion.3.row_at_ref, s32[4]{0:T(128)} %and_select_fusion.2.col_at_ref, f32[16,6,6,16,256]{4,3,2,1,0:T(8,128)} %bitcast.196, f32[4,2,6,3,32,256]{5,4,3,2,1,0:T(8,128)} %all-to-all-done.2.refs_0_, bf16[15,256,256]{2,1,0:T(8,128)(2,1)} %copy-done, ...), custom_call_target="tpu_custom_call" | custom-call | tf_op jit(solution)/shard_map/finish/pallas_call | solution.py:299
  (24 shorter events, 0.2 us)
Async XLA Ops:
  6.5 159.0 %all-gather.7.cloned.1.call-start = ((), (), s32[]{:S(2)}) async-start(), calls=%async_computation.4 | async-start | bytes 5849088 | tf_op jit(solution)/shard_map/all_gather | solution.py:389
  6.5 2.6 copy-start.9
  6.5 15.9 %copy-start.8 = (f32[12288]{0:T(1024)S(1)}, f32[12288]{0:T(1024)}, u32[]{:S(2)}) copy-start(f32[12288]{0:T(1024)} %param.5) | copy-start | bytes 147460
  8.3 14.2 %collective-permute-start = (f32[4,256,256]{2,1,0:T(8,128)S(1)}, f32[4,256,256]{2,1,0:T(8,128)S(1)}, u32[]{:S(2)}, u32[]{:S(2)}) collective-permute-start(f32[4,256,256]{2,1,0:T(8,128)S(1)} %get-tuple-element.27), channel_id=1, source_target_pairs={{0,64},{1,65},{2,66},{3,67},{4,68},{5,69},{16,80},{17,81},{18,82},... | collective-permute-start | bytes 3145736 | tf_op jit(solution)/shard_map/ppermute | solution.py:326
  86.6 0.8 copy-start.7
  87.4 150.3 %all-gather.5.cloned.1.call-start = ((), (), s32[]{:S(2)}) async-start(), calls=%async_computation.3 | async-start | bytes 10027008 | tf_op jit(solution)/shard_map/all_gather | solution.py:416
  89.0 2.8 copy-start.6
  91.8 19.2 %collective-permute-start.3 = (f32[6,3,16,256]{3,2,1,0:T(8,128)S(1)}, f32[6,3,16,256]{3,2,1,0:T(8,128)S(1)}, u32[]{:S(2)}, u32[]{:S(2)}) collective-permute-start(f32[6,3,16,256]{3,2,1,0:T(8,128)S(1)} %get-tuple-element.32), channel_id=1, source_target_pairs={{0,72},{1,64},{2,88},{3,80},{4,104},{5,96},{6,120},{7,112},{8,8},{... | collective-permute-start | bytes 884744 | tf_op jit(solution)/shard_map/ppermute | solution.py:326
  93.8 17.5 %collective-permute-start.4 = (f32[6,3,16,256]{3,2,1,0:T(8,128)S(1)}, f32[6,3,16,256]{3,2,1,0:T(8,128)}, u32[]{:S(2)}, u32[]{:S(2)}) collective-permute-start(f32[6,3,16,256]{3,2,1,0:T(8,128)S(1)} %get-tuple-element.33), channel_id=1, source_target_pairs={{0,64},{1,72},{2,80},{3,88},{4,96},{5,104},{6,112},{7,120},{8,0},{... | collective-permute-start | bytes 884744 | tf_op jit(solution)/shard_map/ppermute | solution.py:326
  96.3 21.6 %collective-permute-start.1 = (f32[6,3,16,256]{3,2,1,0:T(8,128)S(1)}, f32[6,3,16,256]{3,2,1,0:T(8,128)S(1)}, u32[]{:S(2)}, u32[]{:S(2)}) collective-permute-start(f32[6,3,16,256]{3,2,1,0:T(8,128)S(1)} %get-tuple-element.32), channel_id=1, source_target_pairs={{0,8},{1,0},{2,24},{3,16},{4,40},{5,32},{6,56},{7,48},{8,72},{9,64... | collective-permute-start | bytes 884744 | tf_op jit(solution)/shard_map/ppermute | solution.py:326
  103.1 20.7 %collective-permute-start.2 = (f32[6,3,16,256]{3,2,1,0:T(8,128)S(1)}, f32[6,3,16,256]{3,2,1,0:T(8,128)}, u32[]{:S(2)}, u32[]{:S(2)}) collective-permute-start(f32[6,3,16,256]{3,2,1,0:T(8,128)S(1)} %get-tuple-element.33), channel_id=1, source_target_pairs={{0,0},{1,8},{2,16},{3,24},{4,32},{5,40},{6,48},{7,56},{8,64},{9,72... | collective-permute-start | bytes 884744 | tf_op jit(solution)/shard_map/ppermute | solution.py:326
  109.2 128.4 %collective-permute-start.5 = (f32[4,256,512]{2,1,0:T(8,128)S(1)}, f32[4,256,512]{2,1,0:T(8,128)}, u32[]{:S(2)}, u32[]{:S(2)}) collective-permute-start(f32[4,256,512]{2,1,0:T(8,128)S(1)} %fusion.1), channel_id=1, source_target_pairs={{0,64},{1,65},{2,66},{3,67},{4,68},{5,69},{6,70},{7,71},{8,72},{9,... | collective-permute-start | bytes 6291464 | tf_op jit(solution)/shard_map/ppermute | solution.py:326
  127.8 109.8 %all-to-all-start.2 = ((f32[4,2,6,3,32,256]{5,4,3,2,1,0:T(8,128)}), f32[4,2,6,3,32,256]{5,4,3,2,1,0:T(8,128)}, u32[]{:S(2)}, u32[]{:S(2)}) async-start(f32[4,2,6,3,32,256]{5,4,3,2,1,0:T(8,128)} %broadcast_in_dim.96), calls=%async_computation.2 | async-start | bytes 9437184 | tf_op jit(solution)/shard_map/all_to_all | solution.py:380
  165.5 2.6 copy-start.5
  232.0 1.3 copy-start
  233.3 1.4 copy-start.1
  234.7 1.1 copy-start.2
  235.8 0.9 copy-start.3
  236.7 0.9 copy-start.4
Sparse Core Ops, SparseCore 0:
  87.5 77.9 all-gather.6
  167.2 56.5 all-gather.4

commit v5 on v4

--- a/solution.py
+++ b/solution.py
@@ -158,6 +158,7 @@
     out = pl.pallas_call(
         lambda *refs: top_kernel(first, last, *refs),
         out_shape=shapes,
+        out_specs=[pl.BlockSpec(memory_space=pltpu.VMEM)] * len(shapes),
         scratch_shapes=[
             pltpu.VMEM((PANELS * PANELS, BS, BS), f32),
             pltpu.VMEM((3, LEAF, LEAF), f32),
@@ -382,8 +383,6 @@
     column = jnp.stack([raw_tile(p) for p in range(ROW_SLOTS)], axis=1)
     dealt = lax.all_to_all(column, "col", 0, 0)[:PANELS]
 
-    other = swap_rows(after(leaving(slice(0, 2 * BS)), dealt), HALF_ROWS, range(N_COL))
-
     near = row_gather(dealt[:, 0], range(N_ROW))
     packed = jnp.concatenate([near[i, : i + 1] for i in range(PANELS)], axis=0)
     top = lax.all_gather(packed, "col")
@@ -411,6 +410,8 @@
     pair = jnp.stack(pair)
     col_panel = row_gather(pair, range(HALF_ROWS), range(HALF_ROWS, N_ROW))
 
+    other = swap_rows(after(leaving(slice(0, 2 * BS)), pair), HALF_ROWS, range(N_COL))
+
     row_panel = lax.all_gather(after(dealt, top), "col")
 
     row_panel = lax.all_gather(dealt, "col")

time: 294 us -> 293 us (level)
    all_gather x1, waiting for transfers between devices: 29.2 us -> 21.6 us  [on_device(): top = lax.all_gather(packed, 'col')]
    all_gather x1, waiting for transfers between devices: 0.01 us -> 7.28 us  [on_device(): row_panel = lax.all_gather(dealt, 'col')]
  transfers between devices with their start and end apart: 9 -> 9, of which waited for: 4 -> 5; matrix products, arithmetic and copies ran while one was open for 4% -> 4% of each run, Pallas kernels for 22% -> 22%
where the time goes in v5:
time: 293 us; the launch traced here: 291 us
  Pallas kernels  110 us (38%)
  blocking collectives  60.1 us (21%)
  waiting for transfers between devices  42.5 us (15%)
  starting transfers between devices  25.4 us (9%)
  between operations  25.3 us (9%)
  local copies, waits for them, and re-layouts  14.9 us (5%)
  other arithmetic  12.6 us (4%)
    pallas_call x1, Pallas kernels, top_part(): pl.pallas_call(lambda *refs: top_kernel(first, last, *refs), out_shape=sh...  63.9 us
    pallas_call x1, Pallas kernels, finish(): pl.pallas_call(rows_kernel, grid=(tiles + 1,), in_specs=[smem] * 3 + [pl....  46.4 us
    all_to_all x1, blocking collectives, on_device(): dealt = lax.all_to_all(column, 'col', 0, 0)[:PANELS]  40.2 us
    all_gather x1, waiting for transfers between devices, on_device(): top = lax.all_gather(packed, 'col')  21.6 us
    all_to_all x1, blocking collectives, row_gather(): lax.all_to_all(jnp.broadcast_to(x, (n, *x.shape)), 'row', 0, 0, axis_inde...  19.9 us
    ppermute x6, starting transfers between devices, permute(): return lax.ppermute(x, ('row', 'col'), pairs)  17.8 us
    ppermute x6, waiting for transfers between devices, permute(): return lax.ppermute(x, ('row', 'col'), pairs)  13.6 us
    unnamed x30, local copies, waits for them, and re-layouts  9.06 us
  transfers between devices with their start and end apart: 9, of which 5 were waited for; matrix products, arithmetic and copies ran while one was open for 4% of the time, Pallas kernels for 22%

profile of v5, /device:TPU:10, one launch (start us, length us, event | category | flops | bytes accessed | tf_op | source)
XLA Modules:
  0.0 291.2 jit_solution(2060152303152049215)
XLA Ops:
  6.5 0.0 all-gather.7.cloned.1.call-start
  6.5 0.0 copy-start.9
  6.5 0.0 copy-start.8
  6.5 1.8 slice_select_fusion
  8.3 0.7 collective-permute-start
  9.1 0.1 iota_compare_fusion.1
  9.1 0.0 copy-done.9
  9.2 0.1 select_reduce_fusion
  9.3 0.7 fusion.16
  20.2 0.1 iota_compare_fusion.2
  20.3 0.1 select_reduce_fusion.1
  20.4 0.6 fusion.17
  22.4 0.0 copy-done.8
  22.5 0.0 collective-permute-done
  22.5 1.2 bitcast_add_fusion.4
  23.8 1.3 bitcast_add_fusion
  25.1 1.1 bitcast_add_fusion.8
  26.3 40.2 %all_to_all.15 = f32[16,6,16,256]{3,2,1,0:T(8,128)S(1)} all-to-all(f32[16,6,16,256]{3,2,1,0:T(8,128)S(1)} %constant_dynamic-update-slice_fusion), channel_id=1, replica_groups=mesh['row'=8,'col'=16] {'col'}, dimensions={0} | all-to-all | bytes 3145728 | tf_op jit(solution)/shard_map/all_to_all | solution.py:384
  66.5 0.1 broadcast_in_dim.95
  66.6 19.9 %all_to_all.16 = f32[8,6,16,256]{3,2,1,0:T(8,128)S(1)} all-to-all(f32[8,6,16,256]{3,2,1,0:T(8,128)S(1)} %broadcast_in_dim.95), channel_id=1, replica_groups=mesh['row'=8,'col'=16] {'row'}, dimensions={0} | all-to-all | bytes 1572864 | tf_op jit(solution)/shard_map/all_to_all | solution.py:381
  86.6 0.0 copy-start.7
  86.6 0.7 copy-done.7
  87.3 0.0 all-gather.7.cloned.1.call-update
  87.4 0.0 all-gather.5.cloned.1.call-start
  87.4 0.9 slice.232
  88.3 0.0 all-gather.5.cloned.1.call-update
  88.3 0.1 reduce_sum.23
  88.4 0.1 reduce_sum.25
  88.5 0.5 and_select_fusion.3.row_at_ref
  89.0 0.0 copy-start.6
  89.0 2.8 fusion.1
  91.8 0.0 copy-done.6
  91.8 0.1 slice_select_fusion.2
  91.8 1.9 collective-permute-start.3
  93.8 1.9 collective-permute-start.4
  95.7 0.6 and_select_fusion.2.col_at_ref
  96.3 6.8 %collective-permute-start.1 = (f32[6,3,16,256]{3,2,1,0:T(8,128)S(1)}, f32[6,3,16,256]{3,2,1,0:T(8,128)S(1)}, u32[]{:S(2)}, u32[]{:S(2)}) collective-permute-start(f32[6,3,16,256]{3,2,1,0:T(8,128)S(1)} %get-tuple-element.32), channel_id=1, source_target_pairs={{0,8},{1,0},{2,24},{3,16},{4,40},{5,32},{6,56},{7,48},{8,72},{9,64... | collective-permute-start | bytes 884744 | tf_op jit(solution)/shard_map/ppermute | solution.py:327
  103.1 4.8 %collective-permute-start.2 = (f32[6,3,16,256]{3,2,1,0:T(8,128)S(1)}, f32[6,3,16,256]{3,2,1,0:T(8,128)}, u32[]{:S(2)}, u32[]{:S(2)}) collective-permute-start(f32[6,3,16,256]{3,2,1,0:T(8,128)S(1)} %get-tuple-element.33), channel_id=1, source_target_pairs={{0,0},{1,8},{2,16},{3,24},{4,32},{5,40},{6,48},{7,56},{8,64},{9,72... | collective-permute-start | bytes 884744 | tf_op jit(solution)/shard_map/ppermute | solution.py:327
  107.9 0.7 pad_add_fusion.place_ref
  108.6 0.6 reshape.201.refs_6_
  109.2 0.0 collective-permute-done.3
  109.2 2.1 collective-permute-done.4
  111.3 1.0 broadcast_select_fusion.1
  112.3 5.5 %collective-permute-done.1 = f32[6,3,16,256]{3,2,1,0:T(8,128)S(1)} collective-permute-done((f32[6,3,16,256]{3,2,1,0:T(8,128)S(1)}, f32[6,3,16,256]{3,2,1,0:T(8,128)S(1)}, u32[]{:S(2)}, u32[]{:S(2)}) %collective-permute-start.1) | collective-permute-done | bytes 294944 | tf_op jit(solution)/shard_map/ppermute | solution.py:327
  117.8 6.1 %collective-permute-done.2 = f32[6,3,16,256]{3,2,1,0:T(8,128)} collective-permute-done((f32[6,3,16,256]{3,2,1,0:T(8,128)S(1)}, f32[6,3,16,256]{3,2,1,0:T(8,128)}, u32[]{:S(2)}, u32[]{:S(2)}) %collective-permute-start.2) | collective-permute-done | bytes 294944 | tf_op jit(solution)/shard_map/ppermute | solution.py:327
  123.8 1.0 broadcast_select_fusion.3
  124.8 0.1 maximum_bitcast_fusion
  124.9 0.1 pad_maximum_fusion
  125.0 2.8 broadcast_in_dim.96
  127.8 7.5 %all-to-all-start.2 = ((f32[4,2,6,3,32,256]{5,4,3,2,1,0:T(8,128)}), f32[4,2,6,3,32,256]{5,4,3,2,1,0:T(8,128)}, u32[]{:S(2)}, u32[]{:S(2)}) async-start(f32[4,2,6,3,32,256]{5,4,3,2,1,0:T(8,128)} %broadcast_in_dim.96), calls=%async_computation.2 | async-start | bytes 9437184 | tf_op jit(solution)/shard_map/all_to_all | solution.py:381
  135.3 1.6 collective-permute-start.5
  136.9 21.6 %all-gather.7.cloned.1.call-done = f32[336,16,256]{2,1,0:T(8,128)} async-done(((f32[21,16,256]{2,1,0:T(8,128)}), f32[336,16,256]{2,1,0:T(8,128)}) %all-gather.7.cloned.1.call-update) | async-done | bytes 5505040 | tf_op jit(solution)/shard_map/all_gather | solution.py:388
  158.5 2.6 copy-done.5
  161.1 63.9 %top0.1 = (bf16[15,256,256]{2,1,0:T(8,128)(2,1)S(1)}, bf16[15,256,256]{2,1,0:T(8,128)(2,1)S(1)}, bf16[6,256,256]{2,1,0:T(8,128)(2,1)S(1)}, bf16[6,256,256]{2,1,0:T(8,128)(2,1)S(1)}, f32[6,256,256]{2,1,0:T(8,128)S(1)}) custom-call(f32[16,21,16,256]{3,2,1,0:T(8,128)S(1)} %bitcast.192), custom_call_target="tpu_custom_call" | custom-call | flops 65999998976 | bytes 240000000 | tf_op jit(solution)/shard_map/top0/pallas_call | solution.py:158
  225.0 0.0 copy-start
  225.0 1.3 copy-done
  226.3 1.4 copy-done.1
  227.7 1.1 copy-done.2
  228.8 0.9 copy-done.3
  229.8 0.9 copy-done.4
  230.6 0.0 collective-permute-done.5.refs_8_
  230.6 0.0 all-to-all-done.2.refs_0_
  230.6 7.3 %all-gather.5.cloned.1.call-done = f32[96,6,16,256]{3,2,1,0:T(8,128)} async-done(((f32[6,6,16,256]{3,2,1,0:T(8,128)}), f32[96,6,16,256]{3,2,1,0:T(8,128)}) %all-gather.5.cloned.1.call-update) | async-done | bytes 9437200 | tf_op jit(solution)/shard_map/all_gather | solution.py:417
  237.9 46.4 %finish.1 = f32[1536,768]{1,0:T(8,128)} custom-call(s32[2]{0:T(128)} %pad_add_fusion.place_ref, s32[8]{0:T(128)} %and_select_fusion.3.row_at_ref, s32[4]{0:T(128)} %and_select_fusion.2.col_at_ref, f32[16,6,6,16,256]{4,3,2,1,0:T(8,128)} %bitcast.196, f32[4,2,6,3,32,256]{5,4,3,2,1,0:T(8,128)} %all-to-all-done.2.refs_0_, bf16[15,256,256]{2,1,0:T(8,128)(2,1)} %copy-done, ...), custom_call_target="tpu_custom_call" | custom-call | tf_op jit(solution)/shard_map/finish/pallas_call | solution.py:300
  (24 shorter events, 0.2 us)
Async XLA Ops:
  6.5 152.0 %all-gather.7.cloned.1.call-start = ((), (), s32[]{:S(2)}) async-start(), calls=%async_computation.4 | async-start | bytes 5849088 | tf_op jit(solution)/shard_map/all_gather | solution.py:388
  6.5 2.6 copy-start.9
  6.5 15.9 %copy-start.8 = (f32[12288]{0:T(1024)S(1)}, f32[12288]{0:T(1024)}, u32[]{:S(2)}) copy-start(f32[12288]{0:T(1024)} %param.5) | copy-start | bytes 147460
  8.3 14.2 %collective-permute-start = (f32[4,256,256]{2,1,0:T(8,128)S(1)}, f32[4,256,256]{2,1,0:T(8,128)S(1)}, u32[]{:S(2)}, u32[]{:S(2)}) collective-permute-start(f32[4,256,256]{2,1,0:T(8,128)S(1)} %get-tuple-element.27), channel_id=1, source_target_pairs={{0,64},{1,65},{2,66},{3,67},{4,68},{5,69},{16,80},{17,81},{18,82},... | collective-permute-start | bytes 3145736 | tf_op jit(solution)/shard_map/ppermute | solution.py:327
  86.6 0.8 copy-start.7
  87.4 150.6 %all-gather.5.cloned.1.call-start = ((), (), s32[]{:S(2)}) async-start(), calls=%async_computation.3 | async-start | bytes 10027008 | tf_op jit(solution)/shard_map/all_gather | solution.py:417
  89.0 2.8 copy-start.6
  91.8 17.4 %collective-permute-start.3 = (f32[6,3,16,256]{3,2,1,0:T(8,128)S(1)}, f32[6,3,16,256]{3,2,1,0:T(8,128)S(1)}, u32[]{:S(2)}, u32[]{:S(2)}) collective-permute-start(f32[6,3,16,256]{3,2,1,0:T(8,128)S(1)} %get-tuple-element.32), channel_id=1, source_target_pairs={{0,72},{1,64},{2,88},{3,80},{4,104},{5,96},{6,120},{7,112},{8,8},{... | collective-permute-start | bytes 884744 | tf_op jit(solution)/shard_map/ppermute | solution.py:327
  93.8 17.5 %collective-permute-start.4 = (f32[6,3,16,256]{3,2,1,0:T(8,128)S(1)}, f32[6,3,16,256]{3,2,1,0:T(8,128)}, u32[]{:S(2)}, u32[]{:S(2)}) collective-permute-start(f32[6,3,16,256]{3,2,1,0:T(8,128)S(1)} %get-tuple-element.33), channel_id=1, source_target_pairs={{0,64},{1,72},{2,80},{3,88},{4,96},{5,104},{6,112},{7,120},{8,0},{... | collective-permute-start | bytes 884744 | tf_op jit(solution)/shard_map/ppermute | solution.py:327
  96.3 21.5 %collective-permute-start.1 = (f32[6,3,16,256]{3,2,1,0:T(8,128)S(1)}, f32[6,3,16,256]{3,2,1,0:T(8,128)S(1)}, u32[]{:S(2)}, u32[]{:S(2)}) collective-permute-start(f32[6,3,16,256]{3,2,1,0:T(8,128)S(1)} %get-tuple-element.32), channel_id=1, source_target_pairs={{0,8},{1,0},{2,24},{3,16},{4,40},{5,32},{6,56},{7,48},{8,72},{9,64... | collective-permute-start | bytes 884744 | tf_op jit(solution)/shard_map/ppermute | solution.py:327
  103.1 20.7 %collective-permute-start.2 = (f32[6,3,16,256]{3,2,1,0:T(8,128)S(1)}, f32[6,3,16,256]{3,2,1,0:T(8,128)}, u32[]{:S(2)}, u32[]{:S(2)}) collective-permute-start(f32[6,3,16,256]{3,2,1,0:T(8,128)S(1)} %get-tuple-element.33), channel_id=1, source_target_pairs={{0,0},{1,8},{2,16},{3,24},{4,32},{5,40},{6,48},{7,56},{8,64},{9,72... | collective-permute-start | bytes 884744 | tf_op jit(solution)/shard_map/ppermute | solution.py:327
  127.8 102.8 %all-to-all-start.2 = ((f32[4,2,6,3,32,256]{5,4,3,2,1,0:T(8,128)}), f32[4,2,6,3,32,256]{5,4,3,2,1,0:T(8,128)}, u32[]{:S(2)}, u32[]{:S(2)}) async-start(f32[4,2,6,3,32,256]{5,4,3,2,1,0:T(8,128)} %broadcast_in_dim.96), calls=%async_computation.2 | async-start | bytes 9437184 | tf_op jit(solution)/shard_map/all_to_all | solution.py:381
  135.3 95.4 %collective-permute-start.5 = (f32[4,256,512]{2,1,0:T(8,128)S(1)}, f32[4,256,512]{2,1,0:T(8,128)}, u32[]{:S(2)}, u32[]{:S(2)}) collective-permute-start(f32[4,256,512]{2,1,0:T(8,128)S(1)} %fusion.1), channel_id=1, source_target_pairs={{0,64},{1,65},{2,66},{3,67},{4,68},{5,69},{6,70},{7,71},{8,72},{9,... | collective-permute-start | bytes 6291464 | tf_op jit(solution)/shard_map/ppermute | solution.py:327
  158.5 2.6 copy-start.5
  225.0 1.3 copy-start
  226.3 1.4 copy-start.1
  227.7 1.1 copy-start.2
  228.8 0.9 copy-start.3
  229.8 0.9 copy-start.4
Sparse Core Ops, SparseCore 0:
  87.5 71.0 all-gather.6
  160.2 77.6 all-gather.4
